TPU v7x, 32 devices: a whole 2x2x4 slice. The times are simulated.
32 devices in a mesh: blk: 4 (over z), hub: 4 (over y, x), rep: 2 (over core).
Axes of the slice: x: 2, y: 2, z: 4, core: 2. Of those that a mesh axis runs over, the one named last changes fastest.
Arguments:
- source_feats: bfloat16 [8192, 512], P(('blk', 'hub', 'rep')), may hold values from -6 to 6
- target_feats: bfloat16 [16384, 512], P(('blk', 'hub', 'rep')), may hold values from -6 to 6
- hub_feats: bfloat16 [512, 512], P(('blk', 'hub', 'rep')), may hold values from -6 to 6
- weight_self: bfloat16 [512, 256], replicated, may hold values from -0.25 to 0.25
- weight_neigh: bfloat16 [512, 256], replicated, may hold values from -0.25 to 0.25
- bias_vector: float32 [256], replicated, may hold values from -3 to 3
- send_rows: int32 [32, 4, 32], P(('blk', 'hub', 'rep')), may hold values from 0 to 255
- edge_target: int32 [32, 4096], P(('blk', 'hub', 'rep')), may hold values from 0 to 511
- edge_slot: int32 [32, 4096], P(('blk', 'hub', 'rep')), may hold values from 0 to 255, as said below
- hub_source: int32 [32, 512], P(('blk', 'hub', 'rep')), may hold values from 0 to 255
- hub_target: int32 [32, 512], P(('blk', 'hub', 'rep')), may hold values from 0 to 127
Outputs:
- vertex_out: bfloat16 [16384, 256], P(('blk', 'hub', 'rep'))
- hub_out: bfloat16 [512, 256], P(('blk', 'hub', 'rep'))
Inputs may be any that keep to these rules, and one draw needn't show every extreme that they name: `edge_slot`: A value s < 128 names slot s of table_d (row s % 32 of the block that blk index s // 32 sends); larger values name hubs of the device's blk index. For each device and blk index the slots named lie within a prefix of that block, of uneven length.
All inputs are finite; a program needn't handle non-finite values.
Results may differ from a plain program's by a relative error of at most 0.0025.
Values may be sent and summed in bfloat16 or wider, within the bound.
No kernel may reach another device: no remote copies, remote signals or barrier semaphores. Data moves between devices by JAX's collectives and lax.ppermute only.
A program may use at most 64 MiB of HBM per device.

v0:
```python
import jax
import jax.numpy as jnp
from jax import lax
from jax.sharding import PartitionSpec as P


def on_device(
    source_feats,
    target_feats,
    hub_feats,
    weight_self,
    weight_neigh,
    bias_vector,
    send_rows,
    edge_target,
    edge_slot,
    hub_source,
    hub_target,
):
    width = weight_neigh.shape[1]
    local_proj = jnp.dot(source_feats, weight_neigh, preferred_element_type=jnp.float32).astype(
        jnp.bfloat16
    )
    picked = send_rows[0]
    outgoing = local_proj[picked]
    arrived = lax.all_to_all(outgoing, "blk", split_axis=0, concat_axis=0, tiled=True)
    hub_local = jnp.dot(hub_feats, weight_neigh, preferred_element_type=jnp.float32).astype(
        jnp.bfloat16
    )
    hub_table = lax.all_gather(hub_local, ("hub", "rep"), axis=0, tiled=True)
    group_hubs = lax.axis_size(("hub", "rep")) * hub_feats.shape[0]
    hub_source_rows = local_proj[hub_source[0]]
    hub_select = (
        hub_target[0][None, :] == jnp.arange(group_hubs, dtype=jnp.int32)[:, None]
    ).astype(jnp.bfloat16)
    hub_partial = jnp.dot(hub_select, hub_source_rows, preferred_element_type=jnp.float32)
    hub_edges = jnp.sum(hub_select.astype(jnp.float32), axis=1)
    hub_sum, hub_degree = (
        lax.psum_scatter(hub_partial, ("hub", "rep"), scatter_dimension=0, tiled=True),
        lax.psum_scatter(hub_edges, ("hub", "rep"), scatter_dimension=0, tiled=True),
    )
    table = jnp.concatenate([arrived.reshape(-1, width), hub_table], axis=0)
    gathered = table[edge_slot[0]]
    targets = target_feats.shape[0]
    select = (edge_target[0][None, :] == jnp.arange(targets, dtype=jnp.int32)[:, None]).astype(
        jnp.bfloat16
    )
    neigh_sum = jnp.dot(select, gathered, preferred_element_type=jnp.float32)
    degree = jnp.sum(select.astype(jnp.float32), axis=1)
    own = jnp.dot(target_feats, weight_self, preferred_element_type=jnp.float32)
    vertex_out = jnp.maximum(
        own + neigh_sum / jnp.maximum(degree, 1.0)[:, None] + bias_vector[None, :], 0.0
    ).astype(jnp.bfloat16)
    own_hub = jnp.dot(hub_feats, weight_self, preferred_element_type=jnp.float32)
    hub_out = jnp.maximum(
        own_hub + hub_sum / jnp.maximum(hub_degree, 1.0)[:, None] + bias_vector[None, :], 0.0
    ).astype(jnp.bfloat16)
    return (vertex_out, hub_out)


def solution(mesh):
    in_specs = (
        P(("blk", "hub", "rep"), None),
        P(("blk", "hub", "rep"), None),
        P(("blk", "hub", "rep"), None),
        P(),
        P(),
        P(),
        P(("blk", "hub", "rep"), None, None),
        P(("blk", "hub", "rep"), None),
        P(("blk", "hub", "rep"), None),
        P(("blk", "hub", "rep"), None),
        P(("blk", "hub", "rep"), None),
    )
    out_specs = (P(("blk", "hub", "rep"), None), P(("blk", "hub", "rep"), None))
    return jax.shard_map(
        on_device, mesh=mesh, in_specs=in_specs, out_specs=out_specs, check_vma=False
    )
```

profile of v0, /device:TPU:0, one launch (start us, length us, event | category | flops | bytes accessed | tf_op | source)
XLA Modules:
  0.0 70.3 jit_solution(1386544668343019432)
XLA Ops:
  7.2 0.0 copy-start
  7.2 0.0 copy-start.5
  7.2 0.7 %compare_select_fusion.2 = s32[4,32,1]{1,0,2:T(4,128)S(1)} fusion(s32[1,4,32]{2,1,0:T(4,128)} %param.17), kind=kLoop, calls=%fused_computation.28 | loop fusion | flops 384 | bytes 1024 | tf_op jit(solution)/shard_map/select_n | solution.py:25
  7.9 0.1 reshape.99
  8.0 0.0 copy-start.7
  8.0 0.0 copy-start.1
  8.0 0.0 copy-start.3
  8.1 1.3 %convolution_convert_fusion = bf16[256,256]{1,0:T(8,128)(2,1)S(1)} fusion(bf16[256,512]{1,0:T(8,128)(2,1)} %param.11, bf16[512,256]{1,0:T(8,128)(2,1)} %param.15), kind=kOutput, calls=%fused_computation.13 | convolution fusion | flops 67174400 | bytes 655360 | tf_op jit(solution)/shard_map/dot_general | solution.py:21
  9.4 0.0 copy-start.4
  9.4 0.0 copy-start.8
  9.4 1.5 %gather_fusion = bf16[128,256]{1,0:T(8,128)(2,1)} fusion(bf16[256,256]{1,0:T(8,128)(2,1)S(1)} %convolution_convert_fusion, s32[1024]{0:T(1024)S(1)} %pad_clamp_fusion.1), kind=kCustom, calls=%fused_computation | custom fusion | bytes 131584 | tf_op jit(solution)/shard_map/gather | solution.py:25
  10.9 6.3 %all-to-all-start = ((bf16[4,32,256]{2,1,0:T(8,128)(2,1)}), bf16[4,32,256]{2,1,0:T(8,128)(2,1)S(1)}, u32[]{:S(2)}, u32[]{:S(2)}) async-start(bf16[4,32,256]{2,1,0:T(8,128)(2,1)} %bitcast.2), calls=%async_computation | async-start | bytes 131072 | tf_op jit(solution)/shard_map/all_to_all | solution.py:26
  17.2 0.0 reduce-scatter.2.cloned.1.call-start
  17.2 0.7 compare_select_fusion.1
  17.9 2.0 %gather_fusion.2 = bf16[512,256]{1,0:T(8,128)(2,1)S(1)} fusion(bf16[256,256]{1,0:T(8,128)(2,1)S(1)} %convolution_convert_fusion, s32[1024]{0:T(1024)S(1)} %pad_clamp_fusion), kind=kCustom, calls=%fused_computation.2 | custom fusion | bytes 526336 | tf_op jit(solution)/shard_map/gather | solution.py:32
  19.9 0.0 copy-done.5
  19.9 0.8 %fusion.11 = f32[128,256]{1,0:T(8,128)} fusion(bf16[512,256]{1,0:T(8,128)(2,1)S(1)} %gather_fusion.2, s32[512]{0:T(512)S(1)} %bitcast.27), kind=kOutput, calls=%fused_computation.22 | convolution fusion | flops 33619968 | bytes 395264 | tf_op jit(solution)/shard_map/dot_general | solution.py:36
  20.7 0.0 reduce-scatter.2.cloned.1.call-update
  20.8 0.1 convert_reduce_fusion.1
  20.9 13.4 %all-reduce = f32[128]{0:T(128)S(1)} all-reduce(f32[128]{0:T(128)S(1)} %convert_reduce_fusion.1), channel_id=3, replica_groups=mesh['blk'=4,'hub'=4,'rep'=2] {'hub','rep'}, use_global_device_ids=true, to_apply=%region_3.0.clone | all-reduce | flops 128 | bytes 1024
  34.3 0.0 copy-done.7
  34.3 0.9 %convert_reduce_fusion = f32[512]{0:T(512)S(1)} fusion(s32[4096]{0:T(1024)S(1)} %bitcast.30), kind=kLoop, calls=%fused_computation.3 | loop fusion | flops 8388096 | bytes 18432 | tf_op jit(solution)/shard_map/reduce_sum | solution.py:49
  35.2 0.0 copy-done.1
  35.2 0.0 copy-done.3
  35.2 0.1 convolution_convert_fusion.1
  35.4 0.0 copy-done.4
  35.4 8.2 %all_gather.3 = bf16[128,256]{1,0:T(8,128)(2,1)S(1)} all-gather(bf16[16,256]{1,0:T(8,128)(2,1)S(1)} %convolution_convert_fusion.1), channel_id=1, replica_groups=mesh['blk'=4,'hub'=4,'rep'=2] {'hub','rep'}, dimensions={0}, use_global_device_ids=true | all-gather | bytes 73728 | tf_op jit(solution)/shard_map/all_gather | solution.py:30
  43.6 0.0 copy-done.8
  43.6 0.6 dynamic-slice
  44.9 0.1 dynamic-slice_maximum_fusion
  45.0 0.0 all-to-all-done
  45.0 14.6 %gather_fusion.1 = bf16[4096,256]{1,0:T(8,128)(2,1)S(1)} fusion(bf16[256,256]{1,0:T(8,128)(2,1)S(1)} %pad_maximum_fusion, s32[4096]{0:T(1024)S(1)} %broadcast_clamp_fusion), kind=kCustom, calls=%fused_computation.1 | custom fusion | bytes 4210688 | tf_op jit(solution)/shard_map/gather | solution.py:43
  59.6 0.0 copy-start.2
  59.6 0.0 copy-start.6
  59.6 1.4 %fusion.6 = f32[512,256]{1,0:T(8,128)S(1)} fusion(bf16[4096,256]{1,0:T(8,128)(2,1)S(1)} %gather_fusion.1, s32[4096]{0:T(1024)S(1)} %bitcast.31, f32[512]{0:T(512)S(1)} %broadcast_maximum_fusion), kind=kOutput, calls=%fused_computation.12 | convolution fusion | flops 1075970048 | bytes 2639872 | tf_op jit(solution)/shard_map/dot_general | solution.py:48
  61.0 0.0 copy-done
  61.0 0.0 copy-done.2
  61.0 0.0 copy-done.6
  61.0 1.0 %fusion.5 = bf16[512,256]{1,0:T(8,128)(2,1)} fusion(f32[512,256]{1,0:T(8,128)S(1)} %fusion.6, bf16[512,512]{1,0:T(8,128)(2,1)S(1)} %copy-done, bf16[512,256]{1,0:T(8,128)(2,1)S(1)} %copy-done.2, f32[256]{0:T(256)S(1)} %copy-done.6), kind=kOutput, calls=%fused_computation.11 | convolution fusion | flops 134742016 | bytes 1573888 | tf_op jit(solution)/shard_map/dot_general | solution.py:50
  62.0 0.0 reduce-scatter.2.cloned.1.call-done
  62.0 1.5 %fusion.9 = bf16[16,256]{1,0:T(8,128)(2,1)} fusion(bf16[16,512]{1,0:T(8,128)(2,1)S(1)} %copy-done.3, bf16[512,256]{1,0:T(8,128)(2,1)S(1)} %copy-done.2, f32[16,256]{1,0:T(8,128)} %reduce-scatter.2.cloned.1.call-done, f32[256]{0:T(256)S(1)} %copy-done.6, f32[16]{0:T(128)S(1)} %dynamic-slice_maximum_fusion), kind=kOutput, calls=%fused_computation.17 | convolution fusion | flops 4214784 | bytes 304192 | tf_op jit(solution)/shard_map/dot_general | solution.py:54
  (6 shorter events, 0.1 us)
Async XLA Ops:
  7.2 53.8 %copy-start = (bf16[512,512]{1,0:T(8,128)(2,1)S(1)}, bf16[512,512]{1,0:T(8,128)(2,1)}, u32[]{:S(2)}) copy-start(bf16[512,512]{1,0:T(8,128)(2,1)} %param.12) | copy-start | bytes 1572868
  7.2 12.7 %copy-start.5 = (s32[1,512]{1,0:T(1,128)S(1)}, s32[1,512]{1,0:T(1,128)}, u32[]{:S(2)}) copy-start(s32[1,512]{1,0:T(1,128)} %param.21) | copy-start | bytes 6148
  8.0 26.2 %copy-start.7 = (s32[1,4096]{1,0:T(1,128)S(1)}, s32[1,4096]{1,0:T(1,128)}, u32[]{:S(2)}) copy-start(s32[1,4096]{1,0:T(1,128)} %param.18) | copy-start | bytes 49156
  8.0 27.2 %copy-start.1 = (bf16[512,256]{1,0:T(8,128)(2,1)S(1)}, bf16[512,256]{1,0:T(8,128)(2,1)}, u32[]{:S(2)}) copy-start(bf16[512,256]{1,0:T(8,128)(2,1)} %param.15) | copy-start | bytes 786436
  8.0 27.2 %copy-start.3 = (bf16[16,512]{1,0:T(8,128)(2,1)S(1)}, bf16[16,512]{1,0:T(8,128)(2,1)}, u32[]{:S(2)}) copy-start(bf16[16,512]{1,0:T(8,128)(2,1)} %param.13) | copy-start | bytes 49156
  9.4 26.0 %copy-start.4 = (s32[1,4096]{1,0:T(1,128)S(1)}, s32[1,4096]{1,0:T(1,128)}, u32[]{:S(2)}) copy-start(s32[1,4096]{1,0:T(1,128)} %param.19) | copy-start | bytes 49156
  9.4 34.3 %copy-start.8 = (u32[32]{0:T(128)S(1)}, u32[32]{0:T(128)}, u32[]{:S(2)}) copy-start(u32[32]{0:T(128)} %constant.23) | copy-start | bytes 388
  10.9 34.1 %all-to-all-start = ((bf16[4,32,256]{2,1,0:T(8,128)(2,1)}), bf16[4,32,256]{2,1,0:T(8,128)(2,1)S(1)}, u32[]{:S(2)}, u32[]{:S(2)}) async-start(bf16[4,32,256]{2,1,0:T(8,128)(2,1)} %bitcast.2), calls=%async_computation | async-start | bytes 131072 | tf_op jit(solution)/shard_map/all_to_all | solution.py:26
  17.2 44.8 %reduce-scatter.2.cloned.1.call-start = ((), (), s32[]{:S(2)}) async-start(), calls=%async_computation.2 | async-start | bytes 147456 | tf_op jit(solution)/shard_map/reduce_scatter | solution.py:39
  59.6 1.4 %copy-start.2 = (bf16[512,256]{1,0:T(8,128)(2,1)S(1)}, bf16[512,256]{1,0:T(8,128)(2,1)}, u32[]{:S(2)}) copy-start(bf16[512,256]{1,0:T(8,128)(2,1)} %param.14) | copy-start | bytes 786436
  59.6 1.4 %copy-start.6 = (f32[256]{0:T(256)S(1)}, f32[256]{0:T(256)}, u32[]{:S(2)}) copy-start(f32[256]{0:T(256)} %param.16) | copy-start | bytes 3076
Sparse Core Ops, SparseCore 0:
  21.0 34.9 reduce-scatter.1
where the time goes:
time: 70.8 us; the launch traced here: 70.3 us
  blocking collectives  21.6 us (31%)
  local copies, waits for them, and re-layouts  18.8 us (27%)
  between operations  14.8 us (21%)
  starting transfers between devices  6.35 us (9%)
  matrix products  6.13 us (9%)
  other arithmetic  2.59 us (4%)
    gather x1, local copies, waits for them, and re-layouts, on_device(): gathered = table[edge_slot[0]]  14.6 us
    unnamed x1, blocking collectives  13.4 us
    all_gather x1, blocking collectives, on_device(): hub_table = lax.all_gather(hub_local, ('hub', 'rep'), axis=0, tiled=True)  8.25 us
    all_to_all x1, starting transfers between devices, on_device(): lax.all_to_all(outgoing, 'blk', split_axis=0, concat_axis=0, tiled=True)  6.35 us
    gather x1, local copies, waits for them, and re-layouts, on_device(): hub_source_rows = local_proj[hub_source[0]]  1.95 us
    gather x1, local copies, waits for them, and re-layouts, on_device(): outgoing = local_proj[picked]  1.48 us
    dot_general x1, matrix products, on_device(): jnp.dot(hub_feats, weight_self, preferred_element_type=jnp.float32)  1.47 us
  transfers between devices with their start and end apart: 2, of which 0 were waited for; matrix products, arithmetic and copies ran while one was open for 32% of the time, Pallas kernels for 0%

commit v1 on v0

v1 whole, which is shorter than its diff:
```python
import functools

import jax
import jax.numpy as jnp
from jax import lax
from jax.experimental import pallas as pl
from jax.experimental.pallas import tpu as pltpu
from jax.sharding import PartitionSpec as P

GROUP = ("hub", "rep")
F32 = jnp.float32
BF16 = jnp.bfloat16
COUNT_ROWS = 8


def bits_of(size):
    bits = size.bit_length() - 1
    assert size == 1 << bits
    return bits


def reverse_bits(value, bits):
    out = jnp.zeros_like(value)
    for i in range(bits):
        out = out | (((value >> i) & 1) << (bits - 1 - i))
    return out


def one_hot(ids, rows):
    lane = lax.broadcasted_iota(jnp.int32, (rows, ids.shape[1]), 0)
    return jnp.where(lane == ids, 1.0, 0.0).astype(BF16)


def dot_tn(a, b):
    return lax.dot_general(a, b, (((0,), (0,)), ((), ())), preferred_element_type=F32)


def dot_nt(a, b):
    return lax.dot_general(a, b, (((1,), (1,)), ((), ())), preferred_element_type=F32)


def project_kernel(
    members, peers, place, src, hub, w, send, h_src, h_tgt, out, keep, move, cnt, hubs
):
    proj = jnp.dot(src[...], w[...], preferred_element_type=F32).astype(BF16)
    hubs[...] = jnp.dot(hub[...], w[...], preferred_element_type=F32).astype(BF16).astype(F32)
    sources = src.shape[0]
    cap = send.shape[1]
    for k in range(peers):
        row = send[pl.ds(place[0] ^ k, 1), :]
        out[pl.ds(k * cap, cap), :] = dot_tn(one_hot(row, sources), proj).astype(BF16)
    picked = dot_tn(one_hot(h_src[...], sources), proj).astype(BF16)
    per = hub.shape[0]
    total = members * per
    shift = bits_of(per)
    target = h_tgt[...]
    owner = reverse_bits((target >> shift) ^ place[1], bits_of(members))
    slot = (owner << shift) | (target & (per - 1))
    partial = jnp.dot(one_hot(slot, total), picked, preferred_element_type=F32)
    keep[...] = partial[: total // 2]
    move[...] = partial[total // 2 :]
    width = w.shape[1]
    ones = jnp.ones((COUNT_ROWS, target.shape[1]), BF16)
    cnt[...] = dot_nt(ones, one_hot(target, width))


def count_kernel(peers, cap, place, tgt_feats, w, bias, e_tgt, e_slot, own, hi, lo, deg):
    own[...] = jnp.dot(tgt_feats[...], w[...], preferred_element_type=F32) + bias[...]
    targets, slots = hi.shape
    edges = e_tgt.shape[1]
    chunk = 512
    base = peers * cap
    raw = e_slot[...]
    slot = jnp.where(raw < base, raw ^ (place[0] * cap), base + ((raw - base) ^ place[2]))
    target = e_tgt[...]
    acc = jnp.zeros((targets, slots), F32)
    for c in range(0, edges, chunk):
        t = one_hot(target[:, c : c + chunk], targets)
        s = one_hot(slot[:, c : c + chunk], slots)
        acc = acc + dot_nt(t, s)
    top = jnp.floor(acc * (1.0 / 256.0))
    hi[...] = top.astype(BF16)
    lo[...] = (acc - 256.0 * top).astype(BF16)
    deg[...] = jnp.maximum(jnp.sum(acc, axis=1, keepdims=True), 1.0)


def finish_kernel(place, hi, lo, own, deg, table, hub, w, bias, sums, cnt, out, hub_out):
    rows = table[...]
    neigh = 256.0 * jnp.dot(hi[...], rows, preferred_element_type=F32) + jnp.dot(
        lo[...], rows, preferred_element_type=F32
    )
    out[...] = jnp.maximum(own[...] + neigh / deg[...], 0.0).astype(BF16)
    mine = jnp.dot(hub[...], w[...], preferred_element_type=F32) + bias[...]
    per = hub.shape[0]
    width = cnt.shape[1]
    r = lax.broadcasted_iota(jnp.int32, (per, width), 0)
    c = lax.broadcasted_iota(jnp.int32, (per, width), 1)
    degree = jnp.sum(
        jnp.where(c == r + place[1] * per, cnt[0:1, :], 0.0), axis=1, keepdims=True
    )
    hub_out[...] = jnp.maximum(mine + sums[...] / jnp.maximum(degree, 1.0), 0.0).astype(BF16)


def call(kernel, out_shape, *args):
    specs = [pl.BlockSpec(memory_space=pltpu.SMEM)]
    specs += [pl.BlockSpec(memory_space=pltpu.VMEM)] * (len(args) - 1)
    return pl.pallas_call(
        kernel,
        out_shape=out_shape,
        in_specs=specs,
        out_specs=jax.tree.map(lambda _: pl.BlockSpec(memory_space=pltpu.VMEM), out_shape),
    )(*args)


def swap(x, axes, size, bit):
    return lax.ppermute(x, axes, [(i, i ^ bit) for i in range(size)])


def on_device(
    source_feats,
    target_feats,
    hub_feats,
    weight_self,
    weight_neigh,
    bias_vector,
    send_rows,
    edge_target,
    edge_slot,
    hub_source,
    hub_target,
):
    shape = jax.ShapeDtypeStruct
    width = weight_neigh.shape[1]
    peers = lax.axis_size("blk")
    members = lax.axis_size(GROUP)
    cap = send_rows.shape[2]
    per = hub_feats.shape[0]
    group_hubs = members * per
    slots = peers * cap + group_hubs
    targets = target_feats.shape[0]
    bias = bias_vector[None, :]
    blk = lax.axis_index("blk")
    member = lax.axis_index(GROUP)
    place = jnp.stack([blk, member, member * per]).astype(jnp.int32)

    half = group_hubs // 2
    outgoing, keep, move, cnt, hubs = call(
        functools.partial(project_kernel, members, peers),
        (
            shape((peers * cap, width), BF16),
            shape((half, width), F32),
            shape((half, width), F32),
            shape((COUNT_ROWS, width), F32),
            shape((per, width), F32),
        ),
        place, source_feats, hub_feats, weight_neigh, send_rows[0], hub_source, hub_target,
    )
    own, hi, lo, deg = call(
        functools.partial(count_kernel, peers, cap),
        (
            shape((targets, width), F32),
            shape((targets, slots), BF16),
            shape((targets, slots), BF16),
            shape((targets, 1), F32),
        ),
        place, target_feats, weight_self, bias, edge_target, edge_slot,
    )

    for i in range(bits_of(members)):
        half = keep.shape[0]
        got = swap(jnp.concatenate([move, cnt, hubs], axis=0), GROUP, members, 1 << i)
        keep = keep + got[:half]
        cnt = cnt + got[half : half + COUNT_ROWS]
        hubs = jnp.concatenate([hubs, got[half + COUNT_ROWS :]], axis=0)
        if half > per:
            keep, move = keep[: half // 2], keep[half // 2 :]

    blocks = [outgoing[k * cap : (k + 1) * cap] for k in range(peers)]
    for i in range(bits_of(peers)):
        moved = [k for k in range(peers) if k >> i & 1]
        got = swap(jnp.concatenate([blocks[k] for k in moved], axis=0), "blk", peers, 1 << i)
        for j, k in enumerate(moved):
            blocks[k] = got[j * cap : (j + 1) * cap]

    table = jnp.concatenate(blocks + [hubs.astype(BF16)], axis=0)
    return call(
        finish_kernel,
        (shape((targets, width), BF16), shape((per, width), BF16)),
        place, hi, lo, own, deg, table, hub_feats, weight_self, bias, keep, cnt,
    )


def solution(mesh):
    split = P(("blk", "hub", "rep"))
    return jax.shard_map(
        on_device,
        mesh=mesh,
        in_specs=(split,) * 3 + (P(),) * 3 + (split,) * 5,
        out_specs=(split, split),
        check_vma=False,
    )
```

time: 70.8 us -> 32.6 us (0.46)
  blocking collectives: 21.6 us -> 0 us
  local copies, waits for them, and re-layouts: 18.8 us -> 3.65 us
  between operations: 14.8 us -> 0.77 us
  Pallas kernels: 0 us -> 8.5 us
  waiting for transfers between devices: 0.02 us -> 8.07 us
  matrix products: 6.13 us -> 0 us
  starting transfers between devices: 6.35 us -> 9.43 us
  other arithmetic: 2.59 us -> 1.86 us
    gather x3 -> x0, local copies, waits for them, and re-layouts: 18 us -> none  [the longest x1 14.6 us: on_device(): gathered = table[edge_slot[0]]]
    unnamed x1 -> x0, blocking collectives: 13.4 us -> none
    ppermute x0 -> x5, starting transfers between devices: none -> 9.43 us  [swap(): return lax.ppermute(x, axes, [(i, i ^ bit) for i in range(size)])]
    pallas_call x0 -> x3, Pallas kernels: none -> 8.5 us  [call(): pl.pallas_call(kernel, out_shape=out_shape, in_specs=specs, out_specs=jax...]
    all_gather x1 -> x0, blocking collectives: 8.25 us -> none  [on_device(): hub_table = lax.all_gather(hub_local, ('hub', 'rep'), axis=0, tiled=True)]
    ppermute x0 -> x5, waiting for transfers between devices: none -> 8.07 us  [swap(): return lax.ppermute(x, axes, [(i, i ^ bit) for i in range(size)])]
    all_to_all x1 -> x0, starting transfers between devices: 6.35 us -> none  [on_device(): lax.all_to_all(outgoing, 'blk', split_axis=0, concat_axis=0, tiled=True)]
    dot_general x6 -> x0, matrix products: 6.13 us -> none  [the longest x1 1.47 us: on_device(): jnp.dot(hub_feats, weight_self, preferred_element_type=jnp.float32)]
  transfers between devices with their start and end apart: 2 -> 5, of which waited for: 0 -> 3; matrix products, arithmetic and copies ran while one was open for 32% -> 0% of each run, Pallas kernels for 0% -> 11%
where the time goes in v1:
time: 32.6 us; the launch traced here: 32.3 us
  starting transfers between devices  9.43 us (29%)
  Pallas kernels  8.5 us (26%)
  waiting for transfers between devices  8.07 us (25%)
  local copies, waits for them, and re-layouts  3.65 us (11%)
  other arithmetic  1.86 us (6%)
  between operations  0.77 us (2%)
    ppermute x5, starting transfers between devices, swap(): return lax.ppermute(x, axes, [(i, i ^ bit) for i in range(size)])  9.43 us
    pallas_call x3, Pallas kernels, call(): pl.pallas_call(kernel, out_shape=out_shape, in_specs=specs, out_specs=jax...  8.5 us
    ppermute x5, waiting for transfers between devices, swap(): return lax.ppermute(x, axes, [(i, i ^ bit) for i in range(size)])  8.07 us
    unnamed x20, local copies, waits for them, and re-layouts  2.11 us
    slice x1, local copies, waits for them, and re-layouts, on_device(): blocks = [outgoing[k * cap:(k + 1) * cap] for k in range(peers)]  0.77 us
    slice x2, local copies, waits for them, and re-layouts, on_device(): keep, move = (keep[:half // 2], keep[half // 2:])  0.75 us
  transfers between devices with their start and end apart: 5, of which 3 were waited for; matrix products, arithmetic and copies ran while one was open for 0% of the time, Pallas kernels for 11%

profile of v1, /device:TPU:0, one launch (start us, length us, event | category | flops | bytes accessed | tf_op | source)
XLA Modules:
  0.0 32.3 jit_solution(11448830308607741944)
XLA Ops:
  0.6 0.6 %pad_add_fusion.place = s32[3]{0:T(128)} fusion(s32[1]{0:T(128)} %bitcast.2, s32[1]{0:T(128)} %bitcast.1, s32[1]{0:T(128)} %bitcast), kind=kLoop, calls=%fused_computation.24 | loop fusion | flops 6 | bytes 24 | tf_op jit(solution)/shard_map/stack | solution.py:144
  1.3 2.5 %shard_map.123 = (bf16[128,256]{1,0:T(8,128)(2,1)}, f32[64,256]{1,0:T(8,128)}, f32[64,256]{1,0:T(8,128)}, f32[8,256]{1,0:T(8,128)}, f32[16,256]{1,0:T(8,128)}) custom-call(s32[3]{0:T(128)} %pad_add_fusion.place, bf16[256,512]{1,0:T(8,128)(2,1)} %src.1, bf16[16,512]{1,0:T(8,128)(2,1)} %hub.3, bf16[512,256]{1,0:T(8,128)(2,1)} %w.4, s32[4,32]{1,0:T(4,128)} %bitcast.7, ...), custom_call_target="tpu_custom_call" | custom-call | tf_op jit(solution)/shard_map/pallas_call | solution.py:107
  3.7 0.8 %fusion.1 = (bf16[32,256]{1,0:T(8,128)(2,1)S(1)}, bf16[32,256]{1,0:T(8,128)(2,1)S(1)}, bf16[32,256]{1,0:T(8,128)(2,1)S(1)}, bf16[256,256]{1,0:T(8,128)(2,1)S(1)}) fusion(bf16[128,256]{1,0:T(8,128)(2,1)} %get-tuple-element.15), kind=kLoop, calls=%fused_computation.25 | loop fusion | bytes 131072 | tf_op jit(solution)/shard_map/slice | solution.py:178
  4.5 3.1 %collective-permute-start = (bf16[64,256]{1,0:T(8,128)(2,1)S(1)}, bf16[64,256]{1,0:T(8,128)(2,1)S(1)}, u32[]{:S(2)}, u32[]{:S(2)}) collective-permute-start(bf16[64,256]{1,0:T(8,128)(2,1)S(1)} %pad_maximum_fusion.2), channel_id=1, source_target_pairs={{0,8},{8,0},{16,24},{24,16},{1,9},{9,1},{17,25},{25,17},{2,10},{10... | collective-permute-start | bytes 98312 | tf_op jit(solution)/shard_map/ppermute | solution.py:116
  7.6 1.9 %collective-permute-done = bf16[64,256]{1,0:T(8,128)(2,1)S(1)} collective-permute-done((bf16[64,256]{1,0:T(8,128)(2,1)S(1)}, bf16[64,256]{1,0:T(8,128)(2,1)S(1)}, u32[]{:S(2)}, u32[]{:S(2)}) %collective-permute-start) | collective-permute-done | bytes 32800 | tf_op jit(solution)/shard_map/ppermute | solution.py:116
  9.5 0.0 copy-start.5
  9.5 0.0 copy-start.2
  9.5 0.0 copy-start.6
  9.5 3.1 %collective-permute-start.1 = (bf16[64,256]{1,0:T(8,128)(2,1)S(1)}, bf16[64,256]{1,0:T(8,128)(2,1)S(1)}, u32[]{:S(2)}, u32[]{:S(2)}) collective-permute-start(bf16[64,256]{1,0:T(8,128)(2,1)S(1)} %pad_maximum_fusion.3), channel_id=1, source_target_pairs={{0,16},{8,24},{16,0},{24,8},{1,17},{9,25},{17,1},{25,9},{2,18},{10... | collective-permute-start | bytes 98312 | tf_op jit(solution)/shard_map/ppermute | solution.py:116
  12.6 0.0 copy-done.5
  12.6 0.0 copy-done.2
  12.6 0.0 copy-done.6
  12.7 0.1 collective-permute-start.2
  12.7 3.6 %shard_map.122 = (f32[512,256]{1,0:T(8,128)}, bf16[512,256]{1,0:T(8,128)(2,1)}, bf16[512,256]{1,0:T(8,128)(2,1)}, f32[512,1]{1,0:T(8,128)}) custom-call(s32[3]{0:T(128)} %pad_add_fusion.place, bf16[512,512]{1,0:T(8,128)(2,1)} %tgt_feats.1, bf16[512,256]{1,0:T(8,128)(2,1)} %w.5, f32[1,256]{1,0:T(1,128)} %bitcast.5, s32[1,4096]{1,0:T(1,128)} %e_tgt.1, ...), custom_call_target="tpu_custom_call" | custom-call | tf_op jit(solution)/shard_map/pallas_call | solution.py:107
  16.3 0.0 copy-start.4
  16.3 0.0 collective-permute-done.1
  16.4 0.0 collective-permute-done.2
  16.4 0.8 %copy-done.4 = f32[64,256]{1,0:T(8,128)S(1)} copy-done((f32[64,256]{1,0:T(8,128)S(1)}, f32[64,256]{1,0:T(8,128)}, u32[]{:S(2)}) %copy-start.4) | copy-done | bytes 65560
  17.2 0.0 copy-start
  17.2 0.6 %copy-done = f32[64,256]{1,0:T(8,128)} copy-done((f32[64,256]{1,0:T(8,128)}, f32[64,256]{1,0:T(8,128)S(1)}, u32[]{:S(2)}) %copy-start) | copy-done | bytes 65560
  17.8 0.0 slice-start
  17.8 0.8 %slice-done = f32[32,256]{1,0:T(8,128)S(1)} async-done(((f32[64,256]{1,0:T(8,128)}), f32[32,256]{1,0:T(8,128)S(1)}, s32[]{:S(2)}) %slice-start) | async-done | bytes 32792 | tf_op jit(solution)/shard_map/slice | solution.py:176
  18.6 0.0 copy-start.1
  18.6 1.6 %collective-permute-start.3 = (f32[72,256]{1,0:T(8,128)S(1)}, f32[72,256]{1,0:T(8,128)S(1)}, u32[]{:S(2)}, u32[]{:S(2)}) collective-permute-start(f32[72,256]{1,0:T(8,128)S(1)} %pad_maximum_fusion.1), channel_id=1, source_target_pairs={{0,2},{1,3},{2,0},{3,1},{4,6},{5,7},{6,4},{7,5},{8,10},{9,11},{10,... | collective-permute-start | bytes 221192 | tf_op jit(solution)/shard_map/ppermute | solution.py:116
  20.1 3.2 %collective-permute-done.3 = f32[72,256]{1,0:T(8,128)S(1)} collective-permute-done((f32[72,256]{1,0:T(8,128)S(1)}, f32[72,256]{1,0:T(8,128)S(1)}, u32[]{:S(2)}, u32[]{:S(2)}) %collective-permute-start.3) | collective-permute-done | bytes 73760 | tf_op jit(solution)/shard_map/ppermute | solution.py:116
  23.3 0.0 copy-done.1
  23.4 1.6 %collective-permute-start.4 = (f32[88,256]{1,0:T(8,128)S(1)}, f32[88,256]{1,0:T(8,128)S(1)}, u32[]{:S(2)}, u32[]{:S(2)}) collective-permute-start(f32[88,256]{1,0:T(8,128)S(1)} %slice_dynamic-update-slice_fusion), channel_id=1, source_target_pairs={{0,4},{1,5},{2,6},{3,7},{4,0},{5,1},{6,2},{7,3},{8,12},{9,13},{10,... | collective-permute-start | bytes 270344 | tf_op jit(solution)/shard_map/ppermute | solution.py:116
  25.0 3.0 %collective-permute-done.4 = f32[88,256]{1,0:T(8,128)S(1)} collective-permute-done((f32[88,256]{1,0:T(8,128)S(1)}, f32[88,256]{1,0:T(8,128)S(1)}, u32[]{:S(2)}, u32[]{:S(2)}) %collective-permute-start.4) | collective-permute-done | bytes 90144 | tf_op jit(solution)/shard_map/ppermute | solution.py:116
  28.0 0.6 %slice_add_fusion.2.sums = f32[16,256]{1,0:T(8,128)} fusion(f32[88,256]{1,0:T(8,128)S(1)} %collective-permute-done.4, f32[32,256]{1,0:T(8,128)S(1)} %slice_add_fusion.1), kind=kLoop, calls=%fused_computation.20 | loop fusion | flops 4096 | bytes 49152 | tf_op jit(solution)/shard_map/add | solution.py:172
  28.6 0.6 %slice_add_fusion.3.cnt = f32[8,256]{1,0:T(8,128)} fusion(f32[88,256]{1,0:T(8,128)S(1)} %collective-permute-done.4, f32[8,256]{1,0:T(8,128)S(1)} %slice_add_fusion.5, f32[72,256]{1,0:T(8,128)S(1)} %collective-permute-done.3), kind=kLoop, calls=%fused_computation.21 | loop fusion | flops 4096 | bytes 32768 | tf_op jit(solution)/shard_map/add | solution.py:173
  29.2 0.0 copy-start.3
  29.2 0.6 %copy-done.3 = bf16[256,256]{1,0:T(8,128)(2,1)} copy-done((bf16[256,256]{1,0:T(8,128)(2,1)}, bf16[256,256]{1,0:T(8,128)(2,1)S(1)}, u32[]{:S(2)}) %copy-start.3) | copy-done | bytes 131096
  29.8 2.5 %shard_map.124 = (bf16[512,256]{1,0:T(8,128)(2,1)}, bf16[16,256]{1,0:T(8,128)(2,1)}) custom-call(s32[3]{0:T(128)} %pad_add_fusion.place, bf16[512,256]{1,0:T(8,128)(2,1)} %get-tuple-element.11.hi, bf16[512,256]{1,0:T(8,128)(2,1)} %get-tuple-element.12.lo, f32[512,256]{1,0:T(8,128)} %get-tuple-element.13.own, f32[512,1]{1,0:T(8,128)} %get-tuple-element.14.deg, ...), custom_call_target="tpu_custom_call" | custom-call | tf_op jit(solution)/shard_map/pallas_call | solution.py:107
  (19 shorter events, 0.1 us)
Async XLA Ops:
  4.5 5.0 %collective-permute-start = (bf16[64,256]{1,0:T(8,128)(2,1)S(1)}, bf16[64,256]{1,0:T(8,128)(2,1)S(1)}, u32[]{:S(2)}, u32[]{:S(2)}) collective-permute-start(bf16[64,256]{1,0:T(8,128)(2,1)S(1)} %pad_maximum_fusion.2), channel_id=1, source_target_pairs={{0,8},{8,0},{16,24},{24,16},{1,9},{9,1},{17,25},{25,17},{2,10},{10... | collective-permute-start | bytes 98312 | tf_op jit(solution)/shard_map/ppermute | solution.py:116
  9.5 3.1 %copy-start.5 = (f32[64,256]{1,0:T(8,128)S(1)}, f32[64,256]{1,0:T(8,128)}, u32[]{:S(2)}) copy-start(f32[64,256]{1,0:T(8,128)} %get-tuple-element.17) | copy-start | bytes 196612
  9.5 3.1 %copy-start.2 = (f32[16,256]{1,0:T(8,128)S(1)}, f32[16,256]{1,0:T(8,128)}, u32[]{:S(2)}) copy-start(f32[16,256]{1,0:T(8,128)} %get-tuple-element.16) | copy-start | bytes 49156
  9.5 3.1 %copy-start.6 = (f32[8,256]{1,0:T(8,128)S(1)}, f32[8,256]{1,0:T(8,128)}, u32[]{:S(2)}) copy-start(f32[8,256]{1,0:T(8,128)} %get-tuple-element.18) | copy-start | bytes 24580
  9.5 6.8 %collective-permute-start.1 = (bf16[64,256]{1,0:T(8,128)(2,1)S(1)}, bf16[64,256]{1,0:T(8,128)(2,1)S(1)}, u32[]{:S(2)}, u32[]{:S(2)}) collective-permute-start(bf16[64,256]{1,0:T(8,128)(2,1)S(1)} %pad_maximum_fusion.3), channel_id=1, source_target_pairs={{0,16},{8,24},{16,0},{24,8},{1,17},{9,25},{17,1},{25,9},{2,18},{10... | collective-permute-start | bytes 98312 | tf_op jit(solution)/shard_map/ppermute | solution.py:116
  12.7 3.7 %collective-permute-start.2 = (f32[88,256]{1,0:T(8,128)S(1)}, f32[88,256]{1,0:T(8,128)S(1)}, u32[]{:S(2)}, u32[]{:S(2)}) collective-permute-start(f32[88,256]{1,0:T(8,128)S(1)} %pad_maximum_fusion), channel_id=1, source_target_pairs={{0,1},{1,0},{2,3},{3,2},{4,5},{5,4},{6,7},{7,6},{8,9},{9,8},{10,11... | collective-permute-start | bytes 270344 | tf_op jit(solution)/shard_map/ppermute | solution.py:116
  16.3 0.8 %copy-start.4 = (f32[64,256]{1,0:T(8,128)S(1)}, f32[64,256]{1,0:T(8,128)}, u32[]{:S(2)}) copy-start(f32[64,256]{1,0:T(8,128)} %get-tuple-element.19) | copy-start | bytes 196612
  17.2 0.6 %copy-start = (f32[64,256]{1,0:T(8,128)}, f32[64,256]{1,0:T(8,128)S(1)}, u32[]{:S(2)}) copy-start(f32[64,256]{1,0:T(8,128)S(1)} %slice_add_fusion) | copy-start | bytes 196612
  17.8 0.8 %slice-start = ((f32[64,256]{1,0:T(8,128)}), f32[32,256]{1,0:T(8,128)S(1)}, s32[]{:S(2)}) async-start(f32[64,256]{1,0:T(8,128)} %copy-done), calls=%async_computation | async-start | bytes 65536 | tf_op jit(solution)/shard_map/slice | solution.py:176
  18.6 4.7 %copy-start.1 = (f32[64,256]{1,0:T(8,128)S(1)}, f32[64,256]{1,0:T(8,128)}, u32[]{:S(2)}) copy-start(f32[64,256]{1,0:T(8,128)} %copy-done) | copy-start | bytes 196612
  18.6 4.7 %collective-permute-start.3 = (f32[72,256]{1,0:T(8,128)S(1)}, f32[72,256]{1,0:T(8,128)S(1)}, u32[]{:S(2)}, u32[]{:S(2)}) collective-permute-start(f32[72,256]{1,0:T(8,128)S(1)} %pad_maximum_fusion.1), channel_id=1, source_target_pairs={{0,2},{1,3},{2,0},{3,1},{4,6},{5,7},{6,4},{7,5},{8,10},{9,11},{10,... | collective-permute-start | bytes 221192 | tf_op jit(solution)/shard_map/ppermute | solution.py:116
  23.4 4.6 %collective-permute-start.4 = (f32[88,256]{1,0:T(8,128)S(1)}, f32[88,256]{1,0:T(8,128)S(1)}, u32[]{:S(2)}, u32[]{:S(2)}) collective-permute-start(f32[88,256]{1,0:T(8,128)S(1)} %slice_dynamic-update-slice_fusion), channel_id=1, source_target_pairs={{0,4},{1,5},{2,6},{3,7},{4,0},{5,1},{6,2},{7,3},{8,12},{9,13},{10,... | collective-permute-start | bytes 270344 | tf_op jit(solution)/shard_map/ppermute | solution.py:116
  29.2 0.7 %copy-start.3 = (bf16[256,256]{1,0:T(8,128)(2,1)}, bf16[256,256]{1,0:T(8,128)(2,1)S(1)}, u32[]{:S(2)}) copy-start(bf16[256,256]{1,0:T(8,128)(2,1)S(1)} %fusion.table) | copy-start | bytes 393220

commit v2 on v1

v2 whole, which is shorter than its diff:
```python
import functools

import jax
import jax.numpy as jnp
from jax import lax
from jax.experimental import pallas as pl
from jax.experimental.pallas import tpu as pltpu
from jax.sharding import PartitionSpec as P

F32 = jnp.float32
BF16 = jnp.bfloat16
COUNT_ROWS = 16
BASE = 256


def bits_of(size):
    bits = size.bit_length() - 1
    assert size == 1 << bits
    return bits


def reverse_bits(value, bits):
    out = value & 0
    for i in range(bits):
        out = out | (((value >> i) & 1) << (bits - 1 - i))
    return out


def one_hot(ids, rows):
    row = lax.broadcasted_iota(jnp.int32, (rows, ids.shape[1]), 0)
    return jnp.where(row == ids, 1.0, 0.0).astype(BF16)


def dot_nn(a, b):
    return jnp.dot(a, b, preferred_element_type=F32)


def dot_nt(a, b):
    return lax.dot_general(a, b, (((1,), (1,)), ((), ())), preferred_element_type=F32)


def split_count(x):
    high = jnp.floor(x * (1.0 / BASE))
    return high.astype(BF16), (x - BASE * high).astype(BF16)


def split_sum(x):
    high = x.astype(BF16)
    return high, (x - high.astype(F32)).astype(BF16)


def places():
    return lax.axis_index("blk"), lax.axis_index("hub"), lax.axis_index("rep")


def pick(core, first, second):
    return jnp.where((core & 1) == 0, first, second)


def project_kernel(
    sizes, src_h, hub_h, w_h, send_h, hs_h, ht_h,
    out, message, keep, cnt,
    src, hub, w, send, hs, ht, lhs, sem,
):
    peers, n_hub, n_rep = sizes
    z, h, c = places()
    copies = [
        pltpu.make_async_copy(a, b, sem.at[i])
        for i, (a, b) in enumerate(
            ((send_h, send), (hs_h, hs), (ht_h, ht), (hub_h, hub), (src_h, src), (w_h, w))
        )
    ]
    for copy in copies:
        copy.start()
    sources = src.shape[0]
    cap = send.shape[2]
    per = hub.shape[0]
    width = w.shape[1]
    total = n_hub * n_rep * per
    half = total // 2
    for copy in copies[:3]:
        copy.wait()
    for p in range(peers):
        k = pick(c, p, reverse_bits(jnp.int32(p), bits_of(peers)))
        row = send[0, pl.ds(k ^ z, 1), :]
        lhs[:, p * cap : (p + 1) * cap] = one_hot(row, sources)
    target = ht[...]
    owner = target >> bits_of(per)
    other = owner & (n_rep - 1)
    x = (owner >> bits_of(n_rep)) ^ h
    order = jnp.where((other & 1) == 0, reverse_bits(x, bits_of(n_hub)), x)
    rep_part = reverse_bits(other ^ c, bits_of(n_rep))
    slot = (((rep_part << bits_of(n_hub)) | order) << bits_of(per)) | (target & (per - 1))
    picks = one_hot(hs[...], sources)
    high, low = split_count(dot_nt(picks, one_hot(slot, total)))
    base = peers * cap
    lhs[:, base : base + total] = low
    lhs[:, base + total :] = high
    ones = jnp.ones((8, target.shape[1]), BF16)
    counts = dot_nt(ones, one_hot(target, width))
    cnt[...] = counts
    high, low = split_count(counts)
    message[2 * half : 2 * half + COUNT_ROWS, :] = jnp.concatenate([high, low], axis=0)
    for copy in copies[3:]:
        copy.wait()
    proj = dot_nn(src[...], w[...]).astype(BF16)
    message[2 * half + COUNT_ROWS :, :] = dot_nn(hub[...], w[...]).astype(BF16)
    got = lax.dot_general(lhs[...], proj, (((0,), (0,)), ((), ())), preferred_element_type=F32)
    out[...] = got[:base].astype(BF16)
    sums = got[base : base + total] + BASE * got[base + total :]
    keep[...] = sums[:half]
    high, low = split_sum(sums[half:])
    message[:half, :] = high
    message[half : 2 * half, :] = low


def merge_kernel(got, sent, kept, cnt, *outs):
    n = kept.shape[0]
    sums = kept[...] + (got[:n].astype(F32) + got[n : 2 * n].astype(F32))
    count_at = 2 * n
    high = got[count_at : count_at + COUNT_ROWS].astype(F32)
    counts = cnt[...] + (BASE * high[:8] + high[8:])
    hubs_at = count_at + COUNT_ROWS
    if len(outs) == 2:
        keep, new_cnt = outs
        keep[...] = sums
        new_cnt[...] = counts
        return
    message, keep, new_cnt = outs
    half = n // 2
    keep[...] = sums[:half]
    new_cnt[...] = counts
    high, low = split_sum(sums[half:])
    message[:half, :] = high
    message[half : 2 * half, :] = low
    high, low = split_count(counts)
    message[2 * half : 2 * half + COUNT_ROWS, :] = jnp.concatenate([high, low], axis=0)
    rows = got.shape[0] - hubs_at
    new_at = 2 * half + COUNT_ROWS
    message[new_at : new_at + rows, :] = sent[hubs_at:, :]
    message[new_at + rows :, :] = got[hubs_at:, :]


def count_kernel(sizes, cap, per, tgt_feats, w, bias, e_tgt, e_slot, own, hi, lo, deg):
    peers, n_hub, n_rep = sizes
    z, h, c = places()
    own[...] = dot_nn(tgt_feats[...], w[...]) + bias[...]
    targets, slots = hi.shape
    edges = e_tgt.shape[1]
    chunk = 512
    base = peers * cap
    raw = e_slot[...]
    k = (raw >> bits_of(cap)) ^ z
    k = jnp.where((c & 1) == 0, k, reverse_bits(k, bits_of(peers)))
    low_slot = (k << bits_of(cap)) | (raw & (cap - 1))
    hub = raw - base
    owner = hub >> bits_of(per)
    x = (owner >> bits_of(n_rep)) ^ h
    x = jnp.where((c & 1) == 0, x, reverse_bits(x, bits_of(n_hub)))
    q = (x << bits_of(n_rep)) | ((owner & (n_rep - 1)) ^ c)
    hub_slot = base + ((q << bits_of(per)) | (hub & (per - 1)))
    slot = jnp.where(raw < base, low_slot, hub_slot)
    target = e_tgt[...]
    acc = jnp.zeros((targets, slots), F32)
    for s in range(0, edges, chunk):
        acc = acc + dot_nt(
            one_hot(target[:, s : s + chunk], targets), one_hot(slot[:, s : s + chunk], slots)
        )
    hi[...], lo[...] = split_count(acc)
    deg[...] = jnp.maximum(jnp.sum(acc, axis=1, keepdims=True), 1.0)


def finish_kernel(
    sizes, hi, lo, own, deg, rows, got, sent, kept, cnt, hub, w, bias, out, hub_out, table
):
    peers, n_hub, n_rep = sizes
    z, h, c = places()
    per = hub.shape[0]
    base = rows.shape[0]
    hubs_at = 2 * per + COUNT_ROWS
    n = got.shape[0] - hubs_at
    table[:base, :] = rows[...]
    table[base : base + n, :] = sent[hubs_at:, :]
    table[base + n :, :] = got[hubs_at:, :]
    values = table[...]
    neigh = BASE * dot_nn(hi[...], values) + dot_nn(lo[...], values)
    out[...] = jnp.maximum(own[...] + neigh / deg[...], 0.0).astype(BF16)
    mine = dot_nn(hub[...], w[...]) + bias[...]
    sums = kept[...] + (got[:per].astype(F32) + got[per : 2 * per].astype(F32))
    high = got[2 * per : 2 * per + COUNT_ROWS].astype(F32)
    counts = cnt[...] + (BASE * high[:8] + high[8:])
    width = cnt.shape[1]
    row = lax.broadcasted_iota(jnp.int32, (per, width), 0)
    lane = lax.broadcasted_iota(jnp.int32, (per, width), 1)
    first = (h * n_rep + c) * per
    degree = jnp.sum(jnp.where(lane == row + first, counts[0:1, :], 0.0), axis=1, keepdims=True)
    hub_out[...] = jnp.maximum(mine + sums / jnp.maximum(degree, 1.0), 0.0).astype(BF16)


def call(name, kernel, out_shape, *args, mib=8, hbm=False, scratch=()):
    spec = pl.BlockSpec(memory_space=pltpu.HBM if hbm else pltpu.VMEM)
    if hbm:
        args = [pltpu.with_memory_space_constraint(a, pltpu.HBM) for a in args]
    with jax.named_scope(name):
        return pl.pallas_call(
            kernel,
            out_shape=out_shape,
            in_specs=[spec] * len(args),
            out_specs=jax.tree.map(lambda _: pl.BlockSpec(memory_space=pltpu.VMEM), out_shape),
            scratch_shapes=scratch,
            compiler_params=pltpu.CompilerParams(vmem_limit_bytes=mib << 20),
            name=name,
        )(*args)


def swap(name, x, axis, size, n_rep, step):
    last = bits_of(size) - 1
    pairs = []
    for i in range(size):
        for c in range(n_rep):
            bit = step if c % 2 == 0 else last - step
            pairs.append((i * n_rep + c, (i ^ (1 << bit)) * n_rep + c))
    with jax.named_scope(name):
        return lax.ppermute(x, (axis, "rep"), pairs)


def on_device(
    source_feats,
    target_feats,
    hub_feats,
    weight_self,
    weight_neigh,
    bias_vector,
    send_rows,
    edge_target,
    edge_slot,
    hub_source,
    hub_target,
):
    shape = jax.ShapeDtypeStruct
    width = weight_neigh.shape[1]
    sizes = tuple(lax.axis_size(a) for a in ("blk", "hub", "rep"))
    peers, n_hub, n_rep = sizes
    assert n_rep == 2
    cap = send_rows.shape[2]
    per = hub_feats.shape[0]
    group_hubs = n_hub * n_rep * per
    assert group_hubs <= width
    slots = peers * cap + group_hubs
    targets = target_feats.shape[0]
    bias = bias_vector[None, :]

    half = group_hubs // 2
    first = [send_rows, hub_source, hub_target, hub_feats, source_feats, weight_neigh]
    outgoing, message, keep, cnt = call(
        "project",
        functools.partial(project_kernel, sizes),
        (
            shape((peers * cap, width), BF16),
            shape((2 * half + COUNT_ROWS + per, width), BF16),
            shape((half, width), F32),
            shape((8, width), F32),
        ),
        source_feats, hub_feats, weight_neigh, send_rows, hub_source, hub_target,
        hbm=True,
        scratch=[
            pltpu.VMEM(a.shape, a.dtype)
            for a in (source_feats, hub_feats, weight_neigh, send_rows, hub_source, hub_target)
        ]
        + [
            pltpu.VMEM((source_feats.shape[0], peers * cap + 2 * group_hubs), BF16),
            pltpu.SemaphoreType.DMA((len(first),)),
        ],
    )

    with jax.named_scope("h0"):
        got = lax.ppermute(message, "rep", [(i, i ^ 1) for i in range(n_rep)])
    for i in range(bits_of(n_hub)):
        half = keep.shape[0] // 2
        rows = got.shape[0] - 2 * keep.shape[0] - COUNT_ROWS
        message, keep, cnt = call(
            f"merge{i}",
            merge_kernel,
            (
                shape((2 * half + COUNT_ROWS + 2 * rows, width), BF16),
                shape((half, width), F32),
                shape((8, width), F32),
            ),
            got, message, keep, cnt,
        )
        got = swap(f"h{i + 1}", message, "hub", n_hub, n_rep, i)

    blocks = [outgoing[k * cap : (k + 1) * cap] for k in range(peers)]
    for i in range(bits_of(peers)):
        moved = [k for k in range(peers) if k >> i & 1]
        arrived = swap(
            f"z{i}", jnp.concatenate([blocks[k] for k in moved], axis=0), "blk", peers, n_rep, i
        )
        for j, k in enumerate(moved):
            blocks[k] = arrived[j * cap : (j + 1) * cap]

    own, hi, lo, deg = call(
        "count",
        functools.partial(count_kernel, sizes, cap, per),
        (
            shape((targets, width), F32),
            shape((targets, slots), BF16),
            shape((targets, slots), BF16),
            shape((targets, 1), F32),
        ),
        target_feats, weight_self, bias, edge_target, edge_slot, mib=24,
    )
    return call(
        "finish",
        functools.partial(finish_kernel, sizes),
        (shape((targets, width), BF16), shape((per, width), BF16)),
        hi, lo, own, deg, jnp.concatenate(blocks, axis=0), got, message, keep, cnt,
        hub_feats, weight_self, bias,
        mib=24 if slots > 1024 else 8,
        scratch=[pltpu.VMEM((slots, width), BF16)],
    )


def solution(mesh):
    split = P(("blk", "hub", "rep"))
    return jax.shard_map(
        on_device,
        mesh=mesh,
        in_specs=(split,) * 3 + (P(),) * 3 + (split,) * 5,
        out_specs=(split, split),
        check_vma=False,
    )
```

time: 32.6 us -> 19.1 us (0.59)
  Pallas kernels: 8.5 us -> 4.29 us
  waiting for transfers between devices: 8.07 us -> 4.33 us
  local copies, waits for them, and re-layouts: 3.65 us -> 0.04 us
  other arithmetic: 1.86 us -> 0.01 us
    pallas_call x3 -> x5, Pallas kernels: 8.5 us -> 4.29 us  [call(): pl.pallas_call(kernel, out_shape=out_shape, in_specs=[spec] * len(args),...]
    ppermute x5, waiting for transfers between devices: 8.07 us -> 4.33 us  [the longest x4 4.33 us: swap(): return lax.ppermute(x, (axis, 'rep'), pairs)]
    unnamed x20 -> x12, local copies, waits for them, and re-layouts: 2.11 us -> 0.03 us
    add x5 -> x0, other arithmetic: 1.21 us -> none  [the longest x3 0.61 us: on_device(): keep = keep + got[:half]]
    slice x1, local copies, waits for them, and re-layouts: 0.77 us -> 0.01 us  [on_device(): blocks = [outgoing[k * cap:(k + 1) * cap] for k in range(peers)]]
    slice x4 -> x1, local copies, waits for them, and re-layouts: 0.76 us -> 0.01 us  [on_device(): blocks[k] = arrived[j * cap:(j + 1) * cap]]
    another operation x1 -> x0, other arithmetic: 0.62 us -> none  [on_device(): place = jnp.stack([blk, member, member * per]).astype(jnp.int32)]
  transfers between devices with their start and end apart: 5 -> 5, of which waited for: 3 -> 2; matrix products, arithmetic and copies ran while one was open for 0% -> 0% of each run, Pallas kernels for 11% -> 8%
where the time goes in v2:
time: 19.1 us; the launch traced here: 19 us
  starting transfers between devices  9.57 us (50%)
  waiting for transfers between devices  4.33 us (23%)
  Pallas kernels  4.29 us (22%)
  between operations  0.72 us (4%)
    ppermute x4, starting transfers between devices, swap(): return lax.ppermute(x, (axis, 'rep'), pairs)  9 us
    ppermute x4, waiting for transfers between devices, swap(): return lax.ppermute(x, (axis, 'rep'), pairs)  4.33 us
    pallas_call x5, Pallas kernels, call(): pl.pallas_call(kernel, out_shape=out_shape, in_specs=[spec] * len(args),...  4.29 us
    ppermute x1, starting transfers between devices, on_device(): got = lax.ppermute(message, 'rep', [(i, i ^ 1) for i in range(n_rep)])  0.57 us
  transfers between devices with their start and end apart: 5, of which 2 were waited for; matrix products, arithmetic and copies ran while one was open for 0% of the time, Pallas kernels for 8%

profile of v2, /device:TPU:0, one launch (start us, length us, event | category | flops | bytes accessed | tf_op | source)
XLA Modules:
  0.0 19.0 jit_solution(3594538718295107358)
XLA Ops:
  0.6 0.0 copy-start.1
  0.6 1.7 %project.1 = (bf16[128,256]{1,0:T(8,128)(2,1)S(1)}, bf16[160,256]{1,0:T(8,128)(2,1)S(1)}, f32[64,256]{1,0:T(8,128)S(1)}, f32[8,256]{1,0:T(8,128)S(1)}) custom-call(bf16[256,512]{1,0:T(8,128)(2,1)} %src_h.1, bf16[16,512]{1,0:T(8,128)(2,1)} %hub.1, bf16[512,256]{1,0:T(8,128)(2,1)} %w_h.1, s32[1,4,32]{2,1,0:T(4,128)} %send_h.1, s32[1,512]{1,0:T(1,128)} %hs_h.1, ...), custom_call_target="tpu_custom_call" | custom-call | tf_op jit(solution)/shard_map/project/project/pallas_call | solution.py:205
  2.4 0.0 copy-start
  2.4 3.1 %collective-permute-start = (bf16[64,256]{1,0:T(8,128)(2,1)S(1)}, bf16[64,256]{1,0:T(8,128)(2,1)S(1)}, u32[]{:S(2)}, u32[]{:S(2)}) collective-permute-start(bf16[64,256]{1,0:T(8,128)(2,1)S(1)} %pad_maximum_fusion.1), channel_id=1, source_target_pairs={{0,8},{1,17},{8,0},{9,25},{16,24},{17,1},{24,16},{25,9},{2,10},{3,... | collective-permute-start | bytes 98312 | tf_op jit(solution)/shard_map/z0/ppermute | solution.py:224
  5.5 0.6 %collective-permute-start.2 = (bf16[160,256]{1,0:T(8,128)(2,1)S(1)}, bf16[160,256]{1,0:T(8,128)(2,1)S(1)}, u32[]{:S(2)}, u32[]{:S(2)}) collective-permute-start(bf16[160,256]{1,0:T(8,128)(2,1)S(1)} %get-tuple-element.21.sent), channel_id=1, source_target_pairs={{0,1},{1,0},{2,3},{3,2},{4,5},{5,4},{6,7},{7,6},{8,9},{9,8},{10,11... | collective-permute-start | bytes 245768 | tf_op jit(solution)/shard_map/h0/ppermute | solution.py:277
  6.1 1.7 %collective-permute-done = bf16[64,256]{1,0:T(8,128)(2,1)S(1)} collective-permute-done((bf16[64,256]{1,0:T(8,128)(2,1)S(1)}, bf16[64,256]{1,0:T(8,128)(2,1)S(1)}, u32[]{:S(2)}, u32[]{:S(2)}) %collective-permute-start) | collective-permute-done | bytes 32800 | tf_op jit(solution)/shard_map/z0/ppermute | solution.py:224
  7.8 0.0 collective-permute-done.2.got
  7.8 1.8 %collective-permute-start.3 = (bf16[112,256]{1,0:T(8,128)(2,1)S(1)}, bf16[112,256]{1,0:T(8,128)(2,1)S(1)}, u32[]{:S(2)}, u32[]{:S(2)}) collective-permute-start(bf16[112,256]{1,0:T(8,128)(2,1)S(1)} %get-tuple-element.24.sent), channel_id=1, source_target_pairs={{0,2},{1,5},{2,0},{3,7},{4,6},{5,1},{6,4},{7,3},{8,10},{9,13},{10,... | collective-permute-start | bytes 172040 | tf_op jit(solution)/shard_map/h1/ppermute | solution.py:224
  9.6 0.0 copy-start.3
  9.6 0.0 copy-start.4
  9.6 0.0 copy-start.5
  9.6 2.5 %collective-permute-start.1 = (bf16[64,256]{1,0:T(8,128)(2,1)S(1)}, bf16[64,256]{1,0:T(8,128)(2,1)S(1)}, u32[]{:S(2)}, u32[]{:S(2)}) collective-permute-start(bf16[64,256]{1,0:T(8,128)(2,1)S(1)} %pad_maximum_fusion.2), channel_id=1, source_target_pairs={{0,16},{1,9},{8,24},{9,1},{16,0},{17,25},{24,8},{25,17},{2,18},{3,... | collective-permute-start | bytes 98312 | tf_op jit(solution)/shard_map/z1/ppermute | solution.py:224
  12.1 0.0 copy-done.1
  12.1 0.0 copy-done
  12.1 0.0 copy-done.3
  12.1 0.0 copy-done.4
  12.1 0.0 copy-done.5
  12.1 1.5 %count.1 = (f32[512,256]{1,0:T(8,128)S(1)}, bf16[512,256]{1,0:T(8,128)(2,1)S(1)}, bf16[512,256]{1,0:T(8,128)(2,1)S(1)}, f32[512,1]{1,0:T(8,128)S(1)}) custom-call(bf16[512,512]{1,0:T(8,128)(2,1)S(1)} %copy-done.1, bf16[512,256]{1,0:T(8,128)(2,1)S(1)} %copy-done, f32[1,256]{1,0:T(1,128)S(1)} %bitcast.1, s32[1,4096]{1,0:T(1,128)S(1)} %copy-done.3, ...), custom_call_target="tpu_custom_call" | custom-call | tf_op jit(solution)/shard_map/count/count/pallas_call | solution.py:205
  13.7 0.0 collective-permute-done.3.got
  13.7 1.6 %collective-permute-start.4 = (bf16[112,256]{1,0:T(8,128)(2,1)S(1)}, bf16[112,256]{1,0:T(8,128)(2,1)S(1)}, u32[]{:S(2)}, u32[]{:S(2)}) collective-permute-start(bf16[112,256]{1,0:T(8,128)(2,1)S(1)} %get-tuple-element.27.sent), channel_id=1, source_target_pairs={{0,4},{1,3},{2,6},{3,1},{4,0},{5,7},{6,2},{7,5},{8,12},{9,11},{10,... | collective-permute-start | bytes 172040 | tf_op jit(solution)/shard_map/h2/ppermute | solution.py:224
  15.3 0.0 collective-permute-done.1
  15.3 0.0 copy-start.2
  15.3 2.6 %collective-permute-done.4.got = bf16[112,256]{1,0:T(8,128)(2,1)S(1)} collective-permute-done((bf16[112,256]{1,0:T(8,128)(2,1)S(1)}, bf16[112,256]{1,0:T(8,128)(2,1)S(1)}, u32[]{:S(2)}, u32[]{:S(2)}) %collective-permute-start.4) | collective-permute-done | bytes 57376 | tf_op jit(solution)/shard_map/h2/ppermute | solution.py:224
  17.9 0.0 copy-done.2
  17.9 1.0 %finish.1 = (bf16[512,256]{1,0:T(8,128)(2,1)}, bf16[16,256]{1,0:T(8,128)(2,1)}) custom-call(bf16[512,256]{1,0:T(8,128)(2,1)S(1)} %get-tuple-element.16.hi, bf16[512,256]{1,0:T(8,128)(2,1)S(1)} %get-tuple-element.17.lo, f32[512,256]{1,0:T(8,128)S(1)} %get-tuple-element.18.own, f32[512,1]{1,0:T(8,128)S(1)} %get-tuple-element.19.deg, ...), custom_call_target="tpu_custom_call" | custom-call | tf_op jit(solution)/shard_map/finish/finish/pallas_call | solution.py:205
  (7 shorter events, 0.1 us)
Async XLA Ops:
  0.6 11.5 %copy-start.1 = (bf16[512,512]{1,0:T(8,128)(2,1)S(1)}, bf16[512,512]{1,0:T(8,128)(2,1)}, u32[]{:S(2)}) copy-start(bf16[512,512]{1,0:T(8,128)(2,1)} %tgt_feats.1) | copy-start | bytes 1572868
  2.4 9.8 %copy-start = (bf16[512,256]{1,0:T(8,128)(2,1)S(1)}, bf16[512,256]{1,0:T(8,128)(2,1)}, u32[]{:S(2)}) copy-start(bf16[512,256]{1,0:T(8,128)(2,1)} %w.3) | copy-start | bytes 786436
  2.4 5.4 %collective-permute-start = (bf16[64,256]{1,0:T(8,128)(2,1)S(1)}, bf16[64,256]{1,0:T(8,128)(2,1)S(1)}, u32[]{:S(2)}, u32[]{:S(2)}) collective-permute-start(bf16[64,256]{1,0:T(8,128)(2,1)S(1)} %pad_maximum_fusion.1), channel_id=1, source_target_pairs={{0,8},{1,17},{8,0},{9,25},{16,24},{17,1},{24,16},{25,9},{2,10},{3,... | collective-permute-start | bytes 98312 | tf_op jit(solution)/shard_map/z0/ppermute | solution.py:224
  5.5 2.3 %collective-permute-start.2 = (bf16[160,256]{1,0:T(8,128)(2,1)S(1)}, bf16[160,256]{1,0:T(8,128)(2,1)S(1)}, u32[]{:S(2)}, u32[]{:S(2)}) collective-permute-start(bf16[160,256]{1,0:T(8,128)(2,1)S(1)} %get-tuple-element.21.sent), channel_id=1, source_target_pairs={{0,1},{1,0},{2,3},{3,2},{4,5},{5,4},{6,7},{7,6},{8,9},{9,8},{10,11... | collective-permute-start | bytes 245768 | tf_op jit(solution)/shard_map/h0/ppermute | solution.py:277
  7.8 5.9 %collective-permute-start.3 = (bf16[112,256]{1,0:T(8,128)(2,1)S(1)}, bf16[112,256]{1,0:T(8,128)(2,1)S(1)}, u32[]{:S(2)}, u32[]{:S(2)}) collective-permute-start(bf16[112,256]{1,0:T(8,128)(2,1)S(1)} %get-tuple-element.24.sent), channel_id=1, source_target_pairs={{0,2},{1,5},{2,0},{3,7},{4,6},{5,1},{6,4},{7,3},{8,10},{9,13},{10,... | collective-permute-start | bytes 172040 | tf_op jit(solution)/shard_map/h1/ppermute | solution.py:224
  9.6 2.6 %copy-start.3 = (s32[1,4096]{1,0:T(1,128)S(1)}, s32[1,4096]{1,0:T(1,128)}, u32[]{:S(2)}) copy-start(s32[1,4096]{1,0:T(1,128)} %e_tgt.1) | copy-start | bytes 49156
  9.6 2.6 %copy-start.4 = (s32[1,4096]{1,0:T(1,128)S(1)}, s32[1,4096]{1,0:T(1,128)}, u32[]{:S(2)}) copy-start(s32[1,4096]{1,0:T(1,128)} %e_slot.1) | copy-start | bytes 49156
  9.6 2.6 %copy-start.5 = (f32[256]{0:T(256)S(1)}, f32[256]{0:T(256)}, u32[]{:S(2)}) copy-start(f32[256]{0:T(256)} %param.16) | copy-start | bytes 3076
  9.6 5.7 %collective-permute-start.1 = (bf16[64,256]{1,0:T(8,128)(2,1)S(1)}, bf16[64,256]{1,0:T(8,128)(2,1)S(1)}, u32[]{:S(2)}, u32[]{:S(2)}) collective-permute-start(bf16[64,256]{1,0:T(8,128)(2,1)S(1)} %pad_maximum_fusion.2), channel_id=1, source_target_pairs={{0,16},{1,9},{8,24},{9,1},{16,0},{17,25},{24,8},{25,17},{2,18},{3,... | collective-permute-start | bytes 98312 | tf_op jit(solution)/shard_map/z1/ppermute | solution.py:224
  13.7 4.2 %collective-permute-start.4 = (bf16[112,256]{1,0:T(8,128)(2,1)S(1)}, bf16[112,256]{1,0:T(8,128)(2,1)S(1)}, u32[]{:S(2)}, u32[]{:S(2)}) collective-permute-start(bf16[112,256]{1,0:T(8,128)(2,1)S(1)} %get-tuple-element.27.sent), channel_id=1, source_target_pairs={{0,4},{1,3},{2,6},{3,1},{4,0},{5,7},{6,2},{7,5},{8,12},{9,11},{10,... | collective-permute-start | bytes 172040 | tf_op jit(solution)/shard_map/h2/ppermute | solution.py:224
  15.3 2.7 %copy-start.2 = (bf16[16,512]{1,0:T(8,128)(2,1)S(1)}, bf16[16,512]{1,0:T(8,128)(2,1)}, u32[]{:S(2)}) copy-start(bf16[16,512]{1,0:T(8,128)(2,1)} %hub.1) | copy-start | bytes 49156

commit v3 on v2

--- a/solution.py
+++ b/solution.py
@@ -7,6 +7,7 @@
 from jax.experimental.pallas import tpu as pltpu
 from jax.sharding import PartitionSpec as P
 
+
 F32 = jnp.float32
 BF16 = jnp.bfloat16
 COUNT_ROWS = 16
@@ -49,8 +50,16 @@
     return high, (x - high.astype(F32)).astype(BF16)
 
 
-def places():
-    return lax.axis_index("blk"), lax.axis_index("hub"), lax.axis_index("rep")
+def parity(value, bits):
+    out = value & 1
+    for i in range(1, bits):
+        out = out ^ ((value >> i) & 1)
+    return out
+
+
+def places(n_hub):
+    z, h, c = lax.axis_index("blk"), lax.axis_index("hub"), lax.axis_index("rep")
+    return z, h, c, c ^ parity(h, bits_of(n_hub))
 
 
 def pick(core, first, second):
@@ -58,16 +67,20 @@
 
 
 def project_kernel(
-    sizes, src_h, hub_h, w_h, send_h, hs_h, ht_h,
-    out, message, keep, cnt,
-    src, hub, w, send, hs, ht, lhs, sem,
+    sizes, src_h, hub_h, w_h, send_h, hs_h, ht_h, et_h, es_h, bias_h,
+    out, message, keep, cnt, et, es, bias, hub,
+    src, w, send, hs, ht, lhs, sem,
 ):
     peers, n_hub, n_rep = sizes
-    z, h, c = places()
+    z, h, c, side = places(n_hub)
     copies = [
         pltpu.make_async_copy(a, b, sem.at[i])
         for i, (a, b) in enumerate(
-            ((send_h, send), (hs_h, hs), (ht_h, ht), (hub_h, hub), (src_h, src), (w_h, w))
+            (
+                (send_h, send), (hs_h, hs), (ht_h, ht),
+                (hub_h, hub), (src_h, src), (w_h, w), (et_h, et), (es_h, es),
+                (bias_h, bias),
+            )
         )
     ]
     for copy in copies:
@@ -86,11 +99,12 @@
         lhs[:, p * cap : (p + 1) * cap] = one_hot(row, sources)
     target = ht[...]
     owner = target >> bits_of(per)
-    other = owner & (n_rep - 1)
-    x = (owner >> bits_of(n_rep)) ^ h
-    order = jnp.where((other & 1) == 0, reverse_bits(x, bits_of(n_hub)), x)
-    rep_part = reverse_bits(other ^ c, bits_of(n_rep))
-    slot = (((rep_part << bits_of(n_hub)) | order) << bits_of(per)) | (target & (per - 1))
+    chip = owner >> 1
+    other = (owner & 1) ^ parity(chip, bits_of(n_hub))
+    x = chip ^ h
+    order = jnp.where(other == 0, reverse_bits(x, bits_of(n_hub)), x)
+    order = order | ((other ^ side) << bits_of(n_hub))
+    slot = (order << bits_of(per)) | (target & (per - 1))
     picks = one_hot(hs[...], sources)
     high, low = split_count(dot_nt(picks, one_hot(slot, total)))
     base = peers * cap
@@ -101,7 +115,7 @@
     cnt[...] = counts
     high, low = split_count(counts)
     message[2 * half : 2 * half + COUNT_ROWS, :] = jnp.concatenate([high, low], axis=0)
-    for copy in copies[3:]:
+    for copy in copies[3:6]:
         copy.wait()
     proj = dot_nn(src[...], w[...]).astype(BF16)
     message[2 * half + COUNT_ROWS :, :] = dot_nn(hub[...], w[...]).astype(BF16)
@@ -112,6 +126,8 @@
     high, low = split_sum(sums[half:])
     message[:half, :] = high
     message[half : 2 * half, :] = low
+    for copy in copies[6:]:
+        copy.wait()
 
 
 def merge_kernel(got, sent, kept, cnt, *outs):
@@ -141,40 +157,52 @@
     message[new_at + rows :, :] = got[hubs_at:, :]
 
 
-def count_kernel(sizes, cap, per, tgt_feats, w, bias, e_tgt, e_slot, own, hi, lo, deg):
-    peers, n_hub, n_rep = sizes
-    z, h, c = places()
-    own[...] = dot_nn(tgt_feats[...], w[...]) + bias[...]
-    targets, slots = hi.shape
-    edges = e_tgt.shape[1]
-    chunk = 512
+def edge_slots(sizes, cap, per, raw):
+    peers, n_hub, _ = sizes
+    z, h, c, side = places(n_hub)
     base = peers * cap
-    raw = e_slot[...]
     k = (raw >> bits_of(cap)) ^ z
     k = jnp.where((c & 1) == 0, k, reverse_bits(k, bits_of(peers)))
     low_slot = (k << bits_of(cap)) | (raw & (cap - 1))
     hub = raw - base
     owner = hub >> bits_of(per)
-    x = (owner >> bits_of(n_rep)) ^ h
-    x = jnp.where((c & 1) == 0, x, reverse_bits(x, bits_of(n_hub)))
-    q = (x << bits_of(n_rep)) | ((owner & (n_rep - 1)) ^ c)
+    chip = owner >> 1
+    x = chip ^ h
+    x = jnp.where(side == 0, x, reverse_bits(x, bits_of(n_hub)))
+    q = (x << 1) | ((owner & 1) ^ parity(chip, bits_of(n_hub)) ^ side)
     hub_slot = base + ((q << bits_of(per)) | (hub & (per - 1)))
-    slot = jnp.where(raw < base, low_slot, hub_slot)
-    target = e_tgt[...]
+    return jnp.where(raw < base, low_slot, hub_slot)
+
+
+def edge_counts(targets, slots, target, slot, first, last):
+    chunk = 512
     acc = jnp.zeros((targets, slots), F32)
-    for s in range(0, edges, chunk):
+    for s in range(first, last, chunk):
         acc = acc + dot_nt(
             one_hot(target[:, s : s + chunk], targets), one_hot(slot[:, s : s + chunk], slots)
         )
-    hi[...], lo[...] = split_count(acc)
-    deg[...] = jnp.maximum(jnp.sum(acc, axis=1, keepdims=True), 1.0)
+    return acc
+
+
+def own_kernel(sizes, cap, per, tgt_feats, w, bias, e_tgt, e_slot, own, acc):
+    own[...] = dot_nn(tgt_feats[...], w[...]) + bias[...]
+    slot = edge_slots(sizes, cap, per, e_slot[...])
+    acc[...] = edge_counts(*acc.shape, e_tgt[...], slot, 0, e_slot.shape[1] // 2)
+
+
+def count_kernel(sizes, cap, per, acc, e_tgt, e_slot, hi, lo, deg):
+    slot = edge_slots(sizes, cap, per, e_slot[...])
+    edges = e_slot.shape[1]
+    counts = acc[...] + edge_counts(*acc.shape, e_tgt[...], slot, edges // 2, edges)
+    hi[...], lo[...] = split_count(counts)
+    deg[...] = jnp.maximum(jnp.sum(counts, axis=1, keepdims=True), 1.0)
 
 
 def finish_kernel(
     sizes, hi, lo, own, deg, rows, got, sent, kept, cnt, hub, w, bias, out, hub_out, table
 ):
-    peers, n_hub, n_rep = sizes
-    z, h, c = places()
+    _, n_hub, n_rep = sizes
+    _, h, c, _ = places(n_hub)
     per = hub.shape[0]
     base = rows.shape[0]
     hubs_at = 2 * per + COUNT_ROWS
@@ -197,31 +225,37 @@
     hub_out[...] = jnp.maximum(mine + sums / jnp.maximum(degree, 1.0), 0.0).astype(BF16)
 
 
-def call(name, kernel, out_shape, *args, mib=8, hbm=False, scratch=()):
+def call(kernel, out_shape, *args, mib=8, hbm=False, scratch=()):
     spec = pl.BlockSpec(memory_space=pltpu.HBM if hbm else pltpu.VMEM)
     if hbm:
         args = [pltpu.with_memory_space_constraint(a, pltpu.HBM) for a in args]
-    with jax.named_scope(name):
-        return pl.pallas_call(
-            kernel,
-            out_shape=out_shape,
-            in_specs=[spec] * len(args),
-            out_specs=jax.tree.map(lambda _: pl.BlockSpec(memory_space=pltpu.VMEM), out_shape),
-            scratch_shapes=scratch,
-            compiler_params=pltpu.CompilerParams(vmem_limit_bytes=mib << 20),
-            name=name,
-        )(*args)
-
-
-def swap(name, x, axis, size, n_rep, step):
-    last = bits_of(size) - 1
+    return pl.pallas_call(
+        kernel,
+        out_shape=out_shape,
+        in_specs=[spec] * len(args),
+        out_specs=jax.tree.map(lambda _: pl.BlockSpec(memory_space=pltpu.VMEM), out_shape),
+        scratch_shapes=scratch,
+        compiler_params=pltpu.CompilerParams(vmem_limit_bytes=mib << 20),
+    )(*args)
+
+
+def swap_hub(x, n_hub, step):
+    bits = bits_of(n_hub)
     pairs = []
-    for i in range(size):
-        for c in range(n_rep):
-            bit = step if c % 2 == 0 else last - step
-            pairs.append((i * n_rep + c, (i ^ (1 << bit)) * n_rep + c))
-    with jax.named_scope(name):
-        return lax.ppermute(x, (axis, "rep"), pairs)
+    for h in range(n_hub):
+        for side in range(2):
+            to = h ^ (1 << (step if side == 0 else bits - 1 - step))
+            pairs.append((2 * h + (side ^ parity(h, bits)), 2 * to + (side ^ parity(to, bits))))
+    return lax.ppermute(x, ("hub", "rep"), pairs)
+
+
+def swap_blk(x, peers, step):
+    pairs = []
+    for z in range(peers):
+        for c in range(2):
+            to = z ^ (1 << (step if c == 0 else bits_of(peers) - 1 - step))
+            pairs.append((2 * z + c, 2 * to + c))
+    return lax.ppermute(x, ("blk", "rep"), pairs)
 
 
 def on_device(
@@ -251,35 +285,36 @@
     bias = bias_vector[None, :]
 
     half = group_hubs // 2
-    first = [send_rows, hub_source, hub_target, hub_feats, source_feats, weight_neigh]
-    outgoing, message, keep, cnt = call(
-        "project",
+    outgoing, message, keep, cnt, e_tgt, e_slot, bias, hubs = call(
         functools.partial(project_kernel, sizes),
         (
             shape((peers * cap, width), BF16),
             shape((2 * half + COUNT_ROWS + per, width), BF16),
             shape((half, width), F32),
             shape((8, width), F32),
+            shape(edge_target.shape, jnp.int32),
+            shape(edge_slot.shape, jnp.int32),
+            shape(bias.shape, F32),
+            shape(hub_feats.shape, BF16),
         ),
         source_feats, hub_feats, weight_neigh, send_rows, hub_source, hub_target,
+        edge_target, edge_slot, bias,
         hbm=True,
         scratch=[
             pltpu.VMEM(a.shape, a.dtype)
-            for a in (source_feats, hub_feats, weight_neigh, send_rows, hub_source, hub_target)
+            for a in (source_feats, weight_neigh, send_rows, hub_source, hub_target)
         ]
         + [
             pltpu.VMEM((source_feats.shape[0], peers * cap + 2 * group_hubs), BF16),
-            pltpu.SemaphoreType.DMA((len(first),)),
+            pltpu.SemaphoreType.DMA((9,)),
         ],
     )
 
-    with jax.named_scope("h0"):
-        got = lax.ppermute(message, "rep", [(i, i ^ 1) for i in range(n_rep)])
+    got = lax.ppermute(message, "rep", [(i, i ^ 1) for i in range(n_rep)])
     for i in range(bits_of(n_hub)):
         half = keep.shape[0] // 2
         rows = got.shape[0] - 2 * keep.shape[0] - COUNT_ROWS
         message, keep, cnt = call(
-            f"merge{i}",
             merge_kernel,
             (
                 shape((2 * half + COUNT_ROWS + 2 * rows, width), BF16),
@@ -288,34 +323,34 @@
             ),
             got, message, keep, cnt,
         )
-        got = swap(f"h{i + 1}", message, "hub", n_hub, n_rep, i)
+        got = swap_hub(message, n_hub, i)
 
     blocks = [outgoing[k * cap : (k + 1) * cap] for k in range(peers)]
     for i in range(bits_of(peers)):
         moved = [k for k in range(peers) if k >> i & 1]
-        arrived = swap(
-            f"z{i}", jnp.concatenate([blocks[k] for k in moved], axis=0), "blk", peers, n_rep, i
-        )
+        arrived = swap_blk(jnp.concatenate([blocks[k] for k in moved], axis=0), peers, i)
         for j, k in enumerate(moved):
             blocks[k] = arrived[j * cap : (j + 1) * cap]
 
-    own, hi, lo, deg = call(
-        "count",
+    own, acc = call(
+        functools.partial(own_kernel, sizes, cap, per),
+        (shape((targets, width), F32), shape((targets, slots), F32)),
+        target_feats, weight_self, bias, e_tgt, e_slot, mib=24,
+    )
+    hi, lo, deg = call(
         functools.partial(count_kernel, sizes, cap, per),
         (
-            shape((targets, width), F32),
             shape((targets, slots), BF16),
             shape((targets, slots), BF16),
             shape((targets, 1), F32),
         ),
-        target_feats, weight_self, bias, edge_target, edge_slot, mib=24,
+        acc, e_tgt, e_slot, mib=24,
     )
     return call(
-        "finish",
         functools.partial(finish_kernel, sizes),
         (shape((targets, width), BF16), shape((per, width), BF16)),
         hi, lo, own, deg, jnp.concatenate(blocks, axis=0), got, message, keep, cnt,
-        hub_feats, weight_self, bias,
+        hubs, weight_self, bias,
         mib=24 if slots > 1024 else 8,
         scratch=[pltpu.VMEM((slots, width), BF16)],
     )
@@ -323,6 +358,7 @@
 
 def solution(mesh):
     split = P(("blk", "hub", "rep"))
+
     return jax.shard_map(
         on_device,
         mesh=mesh,

time: 19.1 us -> 18.1 us (0.948)
  starting transfers between devices: 9.57 us -> 8.16 us
  Pallas kernels: 4.29 us -> 4.55 us
    ppermute x4, starting transfers between devices: 9 us -> 7.59 us  [the longest x2 5.92 us: swap_blk(): return lax.ppermute(x, ('blk', 'rep'), pairs)]
    pallas_call x5 -> x6, Pallas kernels: 4.29 us -> 4.55 us  [call(): pl.pallas_call(kernel, out_shape=out_shape, in_specs=[spec] * len(args),...]
  transfers between devices with their start and end apart: 5 -> 5, of which waited for: 2 -> 2; matrix products, arithmetic and copies ran while one was open for 0% -> 0% of each run, Pallas kernels for 8% -> 10%
where the time goes in v3:
time: 18.1 us; the launch traced here: 18 us
  starting transfers between devices  8.16 us (45%)
  Pallas kernels  4.55 us (25%)
  waiting for transfers between devices  4.51 us (25%)
  between operations  0.71 us (4%)
    ppermute x2, starting transfers between devices, swap_blk(): return lax.ppermute(x, ('blk', 'rep'), pairs)  5.92 us
    pallas_call x6, Pallas kernels, call(): pl.pallas_call(kernel, out_shape=out_shape, in_specs=[spec] * len(args),...  4.55 us
    ppermute x2, waiting for transfers between devices, swap_hub(): return lax.ppermute(x, ('hub', 'rep'), pairs)  2.83 us
    ppermute x2, waiting for transfers between devices, swap_blk(): return lax.ppermute(x, ('blk', 'rep'), pairs)  1.68 us
    ppermute x2, starting transfers between devices, swap_hub(): return lax.ppermute(x, ('hub', 'rep'), pairs)  1.68 us
    ppermute x1, starting transfers between devices, on_device(): got = lax.ppermute(message, 'rep', [(i, i ^ 1) for i in range(n_rep)])  0.57 us
  transfers between devices with their start and end apart: 5, of which 2 were waited for; matrix products, arithmetic and copies ran while one was open for 0% of the time, Pallas kernels for 10%

profile of v3, /device:TPU:0, one launch (start us, length us, event | category | flops | bytes accessed | tf_op | source)
XLA Modules:
  0.0 18.0 jit_solution(7062575922341313594)
XLA Ops:
  0.6 0.0 copy-start.1
  0.6 1.7 %shard_map.122 = (bf16[128,256]{1,0:T(8,128)(2,1)S(1)}, bf16[160,256]{1,0:T(8,128)(2,1)S(1)}, f32[64,256]{1,0:T(8,128)S(1)}, f32[8,256]{1,0:T(8,128)S(1)}, s32[1...) custom-call(bf16[256,512]{1,0:T(8,128)(2,1)} %src_h.1, ...), custom_call_target="tpu_custom_call" | custom-call | tf_op jit(solution)/shard_map/pallas_call | solution.py:232
  2.4 0.0 copy-start
  2.4 3.1 %collective-permute-start = (bf16[64,256]{1,0:T(8,128)(2,1)S(1)}, bf16[64,256]{1,0:T(8,128)(2,1)S(1)}, u32[]{:S(2)}, u32[]{:S(2)}) collective-permute-start(bf16[64,256]{1,0:T(8,128)(2,1)S(1)} %pad_maximum_fusion.1), channel_id=1, source_target_pairs={{0,8},{1,17},{8,0},{9,25},{16,24},{17,1},{24,16},{25,9},{2,10},{3,... | collective-permute-start | bytes 98312 | tf_op jit(solution)/shard_map/ppermute | solution.py:258
  5.6 0.6 %collective-permute-start.2 = (bf16[160,256]{1,0:T(8,128)(2,1)S(1)}, bf16[160,256]{1,0:T(8,128)(2,1)S(1)}, u32[]{:S(2)}, u32[]{:S(2)}) collective-permute-start(bf16[160,256]{1,0:T(8,128)(2,1)S(1)} %get-tuple-element.30.sent), channel_id=1, source_target_pairs={{0,1},{1,0},{2,3},{3,2},{4,5},{5,4},{6,7},{7,6},{8,9},{9,8},{10,11... | collective-permute-start | bytes 245768 | tf_op jit(solution)/shard_map/ppermute | solution.py:313
  6.1 1.7 %collective-permute-done = bf16[64,256]{1,0:T(8,128)(2,1)S(1)} collective-permute-done((bf16[64,256]{1,0:T(8,128)(2,1)S(1)}, bf16[64,256]{1,0:T(8,128)(2,1)S(1)}, u32[]{:S(2)}, u32[]{:S(2)}) %collective-permute-start) | collective-permute-done | bytes 32800 | tf_op jit(solution)/shard_map/ppermute | solution.py:258
  7.8 0.0 collective-permute-done.2.got
  7.8 0.9 %collective-permute-start.3 = (bf16[112,256]{1,0:T(8,128)(2,1)S(1)}, bf16[112,256]{1,0:T(8,128)(2,1)S(1)}, u32[]{:S(2)}, u32[]{:S(2)}) collective-permute-start(bf16[112,256]{1,0:T(8,128)(2,1)S(1)} %get-tuple-element.33.sent), channel_id=1, source_target_pairs={{0,3},{1,4},{3,0},{2,7},{5,6},{4,1},{6,5},{7,2},{8,11},{9,12},{11,... | collective-permute-start | bytes 172040 | tf_op jit(solution)/shard_map/ppermute | solution.py:249
  8.7 2.8 %collective-permute-start.1 = (bf16[64,256]{1,0:T(8,128)(2,1)S(1)}, bf16[64,256]{1,0:T(8,128)(2,1)S(1)}, u32[]{:S(2)}, u32[]{:S(2)}) collective-permute-start(bf16[64,256]{1,0:T(8,128)(2,1)S(1)} %pad_maximum_fusion.2), channel_id=1, source_target_pairs={{0,16},{1,9},{8,24},{9,1},{16,0},{17,25},{24,8},{25,17},{2,18},{3,... | collective-permute-start | bytes 98312 | tf_op jit(solution)/shard_map/ppermute | solution.py:258
  11.5 0.0 copy-done.1
  11.5 0.0 copy-done
  11.5 0.9 %shard_map.123 = (f32[512,256]{1,0:T(8,128)S(1)}, f32[512,256]{1,0:T(8,128)S(1)}) custom-call(bf16[512,512]{1,0:T(8,128)(2,1)S(1)} %copy-done.1, bf16[512,256]{1,0:T(8,128)(2,1)S(1)} %copy-done, f32[1,256]{1,0:T(1,128)S(1)} %get-tuple-element.21.bias, s32[1,4096]{1,0:T(1,128)S(1)} %get-tuple-element.22.e_tgt, s32[1,4096]{1,0:T(1,128)S(1)} %get-tuple-element.23.e_slot), custom_call_target="tpu_custom_call" | custom-call | tf_op jit(solution)/shard_map/pallas_call | solution.py:232
  12.4 0.9 %shard_map.124 = (bf16[512,256]{1,0:T(8,128)(2,1)S(1)}, bf16[512,256]{1,0:T(8,128)(2,1)S(1)}, f32[512,1]{1,0:T(8,128)S(1)}) custom-call(f32[512,256]{1,0:T(8,128)S(1)} %get-tuple-element.24.acc, s32[1,4096]{1,0:T(1,128)S(1)} %get-tuple-element.22.e_tgt, s32[1,4096]{1,0:T(1,128)S(1)} %get-tuple-element.23.e_slot), custom_call_target="tpu_custom_call" | custom-call | tf_op jit(solution)/shard_map/pallas_call | solution.py:232
  13.2 0.0 collective-permute-done.3.got
  13.3 0.8 %collective-permute-start.4 = (bf16[112,256]{1,0:T(8,128)(2,1)S(1)}, bf16[112,256]{1,0:T(8,128)(2,1)S(1)}, u32[]{:S(2)}, u32[]{:S(2)}) collective-permute-start(bf16[112,256]{1,0:T(8,128)(2,1)S(1)} %get-tuple-element.36.sent), channel_id=1, source_target_pairs={{0,5},{1,2},{3,6},{2,1},{5,0},{4,7},{6,3},{7,4},{8,13},{9,10},{11,... | collective-permute-start | bytes 172040 | tf_op jit(solution)/shard_map/ppermute | solution.py:249
  14.1 0.0 collective-permute-done.1
  14.1 2.8 %collective-permute-done.4.got = bf16[112,256]{1,0:T(8,128)(2,1)S(1)} collective-permute-done((bf16[112,256]{1,0:T(8,128)(2,1)S(1)}, bf16[112,256]{1,0:T(8,128)(2,1)S(1)}, u32[]{:S(2)}, u32[]{:S(2)}) %collective-permute-start.4) | collective-permute-done | bytes 57376 | tf_op jit(solution)/shard_map/ppermute | solution.py:249
  16.9 1.0 %shard_map.127 = (bf16[512,256]{1,0:T(8,128)(2,1)}, bf16[16,256]{1,0:T(8,128)(2,1)}) custom-call(bf16[512,256]{1,0:T(8,128)(2,1)S(1)} %get-tuple-element.25.hi, bf16[512,256]{1,0:T(8,128)(2,1)S(1)} %get-tuple-element.26.lo, f32[512,256]{1,0:T(8,128)S(1)} %get-tuple-element.27.own, f32[512,1]{1,0:T(8,128)S(1)} %get-tuple-element.28.deg, ...), custom_call_target="tpu_custom_call" | custom-call | tf_op jit(solution)/shard_map/pallas_call | solution.py:232
  (7 shorter events, 0.1 us)
Async XLA Ops:
  0.6 10.9 %copy-start.1 = (bf16[512,512]{1,0:T(8,128)(2,1)S(1)}, bf16[512,512]{1,0:T(8,128)(2,1)}, u32[]{:S(2)}) copy-start(bf16[512,512]{1,0:T(8,128)(2,1)} %tgt_feats.1) | copy-start | bytes 1572868
  2.4 9.1 %copy-start = (bf16[512,256]{1,0:T(8,128)(2,1)S(1)}, bf16[512,256]{1,0:T(8,128)(2,1)}, u32[]{:S(2)}) copy-start(bf16[512,256]{1,0:T(8,128)(2,1)} %w.3) | copy-start | bytes 786436
  2.4 5.4 %collective-permute-start = (bf16[64,256]{1,0:T(8,128)(2,1)S(1)}, bf16[64,256]{1,0:T(8,128)(2,1)S(1)}, u32[]{:S(2)}, u32[]{:S(2)}) collective-permute-start(bf16[64,256]{1,0:T(8,128)(2,1)S(1)} %pad_maximum_fusion.1), channel_id=1, source_target_pairs={{0,8},{1,17},{8,0},{9,25},{16,24},{17,1},{24,16},{25,9},{2,10},{3,... | collective-permute-start | bytes 98312 | tf_op jit(solution)/shard_map/ppermute | solution.py:258
  5.6 2.3 %collective-permute-start.2 = (bf16[160,256]{1,0:T(8,128)(2,1)S(1)}, bf16[160,256]{1,0:T(8,128)(2,1)S(1)}, u32[]{:S(2)}, u32[]{:S(2)}) collective-permute-start(bf16[160,256]{1,0:T(8,128)(2,1)S(1)} %get-tuple-element.30.sent), channel_id=1, source_target_pairs={{0,1},{1,0},{2,3},{3,2},{4,5},{5,4},{6,7},{7,6},{8,9},{9,8},{10,11... | collective-permute-start | bytes 245768 | tf_op jit(solution)/shard_map/ppermute | solution.py:313
  7.8 5.4 %collective-permute-start.3 = (bf16[112,256]{1,0:T(8,128)(2,1)S(1)}, bf16[112,256]{1,0:T(8,128)(2,1)S(1)}, u32[]{:S(2)}, u32[]{:S(2)}) collective-permute-start(bf16[112,256]{1,0:T(8,128)(2,1)S(1)} %get-tuple-element.33.sent), channel_id=1, source_target_pairs={{0,3},{1,4},{3,0},{2,7},{5,6},{4,1},{6,5},{7,2},{8,11},{9,12},{11,... | collective-permute-start | bytes 172040 | tf_op jit(solution)/shard_map/ppermute | solution.py:249
  8.7 5.4 %collective-permute-start.1 = (bf16[64,256]{1,0:T(8,128)(2,1)S(1)}, bf16[64,256]{1,0:T(8,128)(2,1)S(1)}, u32[]{:S(2)}, u32[]{:S(2)}) collective-permute-start(bf16[64,256]{1,0:T(8,128)(2,1)S(1)} %pad_maximum_fusion.2), channel_id=1, source_target_pairs={{0,16},{1,9},{8,24},{9,1},{16,0},{17,25},{24,8},{25,17},{2,18},{3,... | collective-permute-start | bytes 98312 | tf_op jit(solution)/shard_map/ppermute | solution.py:258
  13.3 3.7 %collective-permute-start.4 = (bf16[112,256]{1,0:T(8,128)(2,1)S(1)}, bf16[112,256]{1,0:T(8,128)(2,1)S(1)}, u32[]{:S(2)}, u32[]{:S(2)}) collective-permute-start(bf16[112,256]{1,0:T(8,128)(2,1)S(1)} %get-tuple-element.36.sent), channel_id=1, source_target_pairs={{0,5},{1,2},{3,6},{2,1},{5,0},{4,7},{6,3},{7,4},{8,13},{9,10},{11,... | collective-permute-start | bytes 172040 | tf_op jit(solution)/shard_map/ppermute | solution.py:249

commit v4 on v3

--- a/solution.py
+++ b/solution.py
@@ -62,13 +62,9 @@
     return z, h, c, c ^ parity(h, bits_of(n_hub))
 
 
-def pick(core, first, second):
-    return jnp.where((core & 1) == 0, first, second)
-
-
 def project_kernel(
-    sizes, src_h, hub_h, w_h, send_h, hs_h, ht_h, et_h, es_h, bias_h,
-    out, message, keep, cnt, et, es, bias, hub,
+    sizes, src_h, hub_h, w_h, send_h, hs_h, ht_h, et_h, es_h, bias_h, tgt_h, ws_h,
+    out, message, keep, cnt, et, es, bias, hub, tgt, ws,
     src, w, send, hs, ht, lhs, sem,
 ):
     peers, n_hub, n_rep = sizes
@@ -78,8 +74,8 @@
         for i, (a, b) in enumerate(
             (
                 (send_h, send), (hs_h, hs), (ht_h, ht),
-                (hub_h, hub), (src_h, src), (w_h, w), (et_h, et), (es_h, es),
-                (bias_h, bias),
+                (src_h, src), (w_h, w), (hub_h, hub), (et_h, et), (es_h, es),
+                (bias_h, bias), (ws_h, ws), (tgt_h, tgt),
             )
         )
     ]
@@ -94,22 +90,22 @@
     for copy in copies[:3]:
         copy.wait()
     for p in range(peers):
-        k = pick(c, p, reverse_bits(jnp.int32(p), bits_of(peers)))
+        k = jnp.where((c & 1) == 1, p, reverse_bits(jnp.int32(p), bits_of(peers)))
         row = send[0, pl.ds(k ^ z, 1), :]
-        lhs[:, p * cap : (p + 1) * cap] = one_hot(row, sources)
+        lhs[p * cap : (p + 1) * cap, :] = one_hot(row, sources).T
     target = ht[...]
     owner = target >> bits_of(per)
     chip = owner >> 1
     other = (owner & 1) ^ parity(chip, bits_of(n_hub))
     x = chip ^ h
-    order = jnp.where(other == 0, reverse_bits(x, bits_of(n_hub)), x)
+    order = jnp.where(other == 1, reverse_bits(x, bits_of(n_hub)), x)
     order = order | ((other ^ side) << bits_of(n_hub))
     slot = (order << bits_of(per)) | (target & (per - 1))
     picks = one_hot(hs[...], sources)
-    high, low = split_count(dot_nt(picks, one_hot(slot, total)))
+    high, low = split_count(dot_nt(one_hot(slot, total), picks))
     base = peers * cap
-    lhs[:, base : base + total] = low
-    lhs[:, base + total :] = high
+    lhs[base : base + total, :] = low
+    lhs[base + total :, :] = high
     ones = jnp.ones((8, target.shape[1]), BF16)
     counts = dot_nt(ones, one_hot(target, width))
     cnt[...] = counts
@@ -119,7 +115,7 @@
         copy.wait()
     proj = dot_nn(src[...], w[...]).astype(BF16)
     message[2 * half + COUNT_ROWS :, :] = dot_nn(hub[...], w[...]).astype(BF16)
-    got = lax.dot_general(lhs[...], proj, (((0,), (0,)), ((), ())), preferred_element_type=F32)
+    got = dot_nn(lhs[...], proj)
     out[...] = got[:base].astype(BF16)
     sums = got[base : base + total] + BASE * got[base + total :]
     keep[...] = sums[:half]
@@ -162,13 +158,13 @@
     z, h, c, side = places(n_hub)
     base = peers * cap
     k = (raw >> bits_of(cap)) ^ z
-    k = jnp.where((c & 1) == 0, k, reverse_bits(k, bits_of(peers)))
+    k = jnp.where((c & 1) == 1, k, reverse_bits(k, bits_of(peers)))
     low_slot = (k << bits_of(cap)) | (raw & (cap - 1))
     hub = raw - base
     owner = hub >> bits_of(per)
     chip = owner >> 1
     x = chip ^ h
-    x = jnp.where(side == 0, x, reverse_bits(x, bits_of(n_hub)))
+    x = jnp.where(side == 1, x, reverse_bits(x, bits_of(n_hub)))
     q = (x << 1) | ((owner & 1) ^ parity(chip, bits_of(n_hub)) ^ side)
     hub_slot = base + ((q << bits_of(per)) | (hub & (per - 1)))
     return jnp.where(raw < base, low_slot, hub_slot)
@@ -190,30 +186,42 @@
     acc[...] = edge_counts(*acc.shape, e_tgt[...], slot, 0, e_slot.shape[1] // 2)
 
 
-def count_kernel(sizes, cap, per, acc, e_tgt, e_slot, hi, lo, deg):
+def count_kernel(sizes, cap, per, acc, e_tgt, e_slot, hi, lo, late, scale):
     slot = edge_slots(sizes, cap, per, e_slot[...])
     edges = e_slot.shape[1]
     counts = acc[...] + edge_counts(*acc.shape, e_tgt[...], slot, edges // 2, edges)
-    hi[...], lo[...] = split_count(counts)
-    deg[...] = jnp.maximum(jnp.sum(counts, axis=1, keepdims=True), 1.0)
-
-
-def finish_kernel(
-    sizes, hi, lo, own, deg, rows, got, sent, kept, cnt, hub, w, bias, out, hub_out, table
-):
+    early = hi.shape[1]
+    high = jnp.floor(counts * (1.0 / BASE))
+    low = counts - BASE * high
+    hi[...] = high[:, :early].astype(BF16)
+    lo[...] = low[:, :early].astype(BF16)
+    span = late.shape[1]
+    lane = lax.broadcasted_iota(jnp.int32, late.shape, 1)
+    moved = pltpu.roll(low[:, -span:], span // 2, 1)
+    late[...] = jnp.where(lane < span // 2, moved, high[:, -span:]).astype(BF16)
+    degree = jnp.maximum(jnp.sum(counts, axis=1, keepdims=True), 1.0)
+    scale[...] = jnp.broadcast_to(1.0 / degree, scale.shape)
+
+
+def blend_kernel(hi, lo, own, scale, rows, sent, hub, w, bias, mean, mine, table):
+    base = rows.shape[0]
+    table[:base, :] = rows[...]
+    table[base:, :] = sent[sent.shape[0] - (table.shape[0] - base) :, :]
+    values = table[...]
+    neigh = BASE * dot_nn(hi[...], values) + dot_nn(lo[...], values)
+    mean[...] = own[...] + neigh * scale[...]
+    mine[...] = dot_nn(hub[...], w[...]) + bias[...]
+
+
+def finish_kernel(sizes, mean, late, scale, got, kept, cnt, mine, out, hub_out):
     _, n_hub, n_rep = sizes
     _, h, c, _ = places(n_hub)
-    per = hub.shape[0]
-    base = rows.shape[0]
+    per = mine.shape[0]
     hubs_at = 2 * per + COUNT_ROWS
-    n = got.shape[0] - hubs_at
-    table[:base, :] = rows[...]
-    table[base : base + n, :] = sent[hubs_at:, :]
-    table[base + n :, :] = got[hubs_at:, :]
-    values = table[...]
-    neigh = BASE * dot_nn(hi[...], values) + dot_nn(lo[...], values)
-    out[...] = jnp.maximum(own[...] + neigh / deg[...], 0.0).astype(BF16)
-    mine = dot_nn(hub[...], w[...]) + bias[...]
+    rows = got[hubs_at:, :]
+    values = jnp.concatenate([rows, (BASE * rows.astype(F32)).astype(BF16)], axis=0)
+    neigh = dot_nn(late[...], values)
+    out[...] = jnp.maximum(mean[...] + neigh * scale[...], 0.0).astype(BF16)
     sums = kept[...] + (got[:per].astype(F32) + got[per : 2 * per].astype(F32))
     high = got[2 * per : 2 * per + COUNT_ROWS].astype(F32)
     counts = cnt[...] + (BASE * high[:8] + high[8:])
@@ -222,7 +230,7 @@
     lane = lax.broadcasted_iota(jnp.int32, (per, width), 1)
     first = (h * n_rep + c) * per
     degree = jnp.sum(jnp.where(lane == row + first, counts[0:1, :], 0.0), axis=1, keepdims=True)
-    hub_out[...] = jnp.maximum(mine + sums / jnp.maximum(degree, 1.0), 0.0).astype(BF16)
+    hub_out[...] = jnp.maximum(mine[...] + sums / jnp.maximum(degree, 1.0), 0.0).astype(BF16)
 
 
 def call(kernel, out_shape, *args, mib=8, hbm=False, scratch=()):
@@ -244,7 +252,7 @@
     pairs = []
     for h in range(n_hub):
         for side in range(2):
-            to = h ^ (1 << (step if side == 0 else bits - 1 - step))
+            to = h ^ (1 << (step if side == 1 else bits - 1 - step))
             pairs.append((2 * h + (side ^ parity(h, bits)), 2 * to + (side ^ parity(to, bits))))
     return lax.ppermute(x, ("hub", "rep"), pairs)
 
@@ -253,7 +261,7 @@
     pairs = []
     for z in range(peers):
         for c in range(2):
-            to = z ^ (1 << (step if c == 0 else bits_of(peers) - 1 - step))
+            to = z ^ (1 << (step if c == 1 else bits_of(peers) - 1 - step))
             pairs.append((2 * z + c, 2 * to + c))
     return lax.ppermute(x, ("blk", "rep"), pairs)
 
@@ -285,7 +293,7 @@
     bias = bias_vector[None, :]
 
     half = group_hubs // 2
-    outgoing, message, keep, cnt, e_tgt, e_slot, bias, hubs = call(
+    outgoing, message, keep, cnt, e_tgt, e_slot, bias, hubs, tgt, w_self = call(
         functools.partial(project_kernel, sizes),
         (
             shape((peers * cap, width), BF16),
@@ -296,17 +304,19 @@
             shape(edge_slot.shape, jnp.int32),
             shape(bias.shape, F32),
             shape(hub_feats.shape, BF16),
+            shape(target_feats.shape, BF16),
+            shape(weight_self.shape, BF16),
         ),
         source_feats, hub_feats, weight_neigh, send_rows, hub_source, hub_target,
-        edge_target, edge_slot, bias,
+        edge_target, edge_slot, bias, target_feats, weight_self,
         hbm=True,
         scratch=[
             pltpu.VMEM(a.shape, a.dtype)
             for a in (source_feats, weight_neigh, send_rows, hub_source, hub_target)
         ]
         + [
-            pltpu.VMEM((source_feats.shape[0], peers * cap + 2 * group_hubs), BF16),
-            pltpu.SemaphoreType.DMA((9,)),
+            pltpu.VMEM((peers * cap + 2 * group_hubs, source_feats.shape[0]), BF16),
+            pltpu.SemaphoreType.DMA((11,)),
         ],
     )
 
@@ -335,24 +345,30 @@
     own, acc = call(
         functools.partial(own_kernel, sizes, cap, per),
         (shape((targets, width), F32), shape((targets, slots), F32)),
-        target_feats, weight_self, bias, e_tgt, e_slot, mib=24,
-    )
-    hi, lo, deg = call(
+        tgt, w_self, bias, e_tgt, e_slot, mib=24,
+    )
+    late_rows = group_hubs // 2
+    hi, lo, late, scale = call(
         functools.partial(count_kernel, sizes, cap, per),
         (
-            shape((targets, slots), BF16),
-            shape((targets, slots), BF16),
-            shape((targets, 1), F32),
+            shape((targets, slots - late_rows), BF16),
+            shape((targets, slots - late_rows), BF16),
+            shape((targets, 2 * late_rows), BF16),
+            shape((targets, width), F32),
         ),
         acc, e_tgt, e_slot, mib=24,
+    )
+    mean, mine = call(
+        blend_kernel,
+        (shape((targets, width), F32), shape((per, width), F32)),
+        hi, lo, own, scale, jnp.concatenate(blocks, axis=0), message, hubs, w_self, bias,
+        mib=24 if slots > 1024 else 8,
+        scratch=[pltpu.VMEM((slots - late_rows, width), BF16)],
     )
     return call(
         functools.partial(finish_kernel, sizes),
         (shape((targets, width), BF16), shape((per, width), BF16)),
-        hi, lo, own, deg, jnp.concatenate(blocks, axis=0), got, message, keep, cnt,
-        hubs, weight_self, bias,
-        mib=24 if slots > 1024 else 8,
-        scratch=[pltpu.VMEM((slots, width), BF16)],
+        mean, late, scale, got, keep, cnt, mine,
     )
 
 

time: 18.1 us -> 19.2 us (1.061); the launches traced: 18 us -> 18.9 us
  starting transfers between devices: 8.16 us -> 9.66 us
  waiting for transfers between devices: 4.51 us -> 3.44 us
  Pallas kernels: 4.55 us -> 5.07 us
    ppermute x2, starting transfers between devices: 1.68 us -> 3.95 us  [swap_hub(): return lax.ppermute(x, ('hub', 'rep'), pairs)]
    ppermute x2, waiting for transfers between devices: 2.83 us -> 1.54 us  [swap_hub(): return lax.ppermute(x, ('hub', 'rep'), pairs)]
    ppermute x1, starting transfers between devices: 0.57 us -> 0.01 us  [on_device(): got = lax.ppermute(message, 'rep', [(i, i ^ 1) for i in range(n_rep)])]
    pallas_call x6 -> x7, Pallas kernels: 4.55 us -> 5.07 us  [call(): pl.pallas_call(kernel, out_shape=out_shape, in_specs=[spec] * len(args),...]
    ppermute x2, waiting for transfers between devices: 1.68 us -> 1.89 us  [swap_blk(): return lax.ppermute(x, ('blk', 'rep'), pairs)]
    ppermute x2, starting transfers between devices: 5.92 us -> 5.71 us  [swap_blk(): return lax.ppermute(x, ('blk', 'rep'), pairs)]
  transfers between devices with their start and end apart: 5 -> 5, of which waited for: 2 -> 2; matrix products, arithmetic and copies ran while one was open for 0% -> 0% of each run, Pallas kernels for 10% -> 13%
where the time goes in v4:
time: 19.2 us; the launch traced here: 18.9 us
  starting transfers between devices  9.66 us (50%)
  Pallas kernels  5.07 us (26%)
  waiting for transfers between devices  3.44 us (18%)
  between operations  0.69 us (4%)
    ppermute x2, starting transfers between devices, swap_blk(): return lax.ppermute(x, ('blk', 'rep'), pairs)  5.71 us
    pallas_call x7, Pallas kernels, call(): pl.pallas_call(kernel, out_shape=out_shape, in_specs=[spec] * len(args),...  5.07 us
    ppermute x2, starting transfers between devices, swap_hub(): return lax.ppermute(x, ('hub', 'rep'), pairs)  3.95 us
    ppermute x2, waiting for transfers between devices, swap_blk(): return lax.ppermute(x, ('blk', 'rep'), pairs)  1.89 us
    ppermute x2, waiting for transfers between devices, swap_hub(): return lax.ppermute(x, ('hub', 'rep'), pairs)  1.54 us
  transfers between devices with their start and end apart: 5, of which 2 were waited for; matrix products, arithmetic and copies ran while one was open for 0% of the time, Pallas kernels for 13%

profile of v4, /device:TPU:0, one launch (start us, length us, event | category | flops | bytes accessed | tf_op | source)
XLA Modules:
  0.0 18.9 jit_solution(5318827940924530819)
XLA Ops:
  0.6 1.7 %shard_map.122 = (bf16[128,256]{1,0:T(8,128)(2,1)S(1)}, bf16[160,256]{1,0:T(8,128)(2,1)S(1)}, f32[64,256]{1,0:T(8,128)S(1)}, f32[8,256]{1,0:T(8,128)S(1)}, s32[1...) custom-call(bf16[256,512]{1,0:T(8,128)(2,1)} %src_h.1, ...), custom_call_target="tpu_custom_call" | custom-call | tf_op jit(solution)/shard_map/pallas_call | solution.py:240
  2.4 4.1 %collective-permute-start = (bf16[64,256]{1,0:T(8,128)(2,1)S(1)}, bf16[64,256]{1,0:T(8,128)(2,1)S(1)}, u32[]{:S(2)}, u32[]{:S(2)}) collective-permute-start(bf16[64,256]{1,0:T(8,128)(2,1)S(1)} %pad_maximum_fusion.1), channel_id=1, source_target_pairs={{0,16},{1,9},{8,24},{9,1},{16,0},{17,25},{24,8},{25,17},{2,18},{3,... | collective-permute-start | bytes 98312 | tf_op jit(solution)/shard_map/ppermute | solution.py:266
  6.5 0.0 collective-permute-start.2
  6.5 1.9 %collective-permute-done = bf16[64,256]{1,0:T(8,128)(2,1)S(1)} collective-permute-done((bf16[64,256]{1,0:T(8,128)(2,1)S(1)}, bf16[64,256]{1,0:T(8,128)(2,1)S(1)}, u32[]{:S(2)}, u32[]{:S(2)}) %collective-permute-start) | collective-permute-done | bytes 32800 | tf_op jit(solution)/shard_map/ppermute | solution.py:266
  8.4 0.0 collective-permute-done.2.got
  8.4 0.7 %collective-permute-start.3 = (bf16[112,256]{1,0:T(8,128)(2,1)S(1)}, bf16[112,256]{1,0:T(8,128)(2,1)S(1)}, u32[]{:S(2)}, u32[]{:S(2)}) collective-permute-start(bf16[112,256]{1,0:T(8,128)(2,1)S(1)} %get-tuple-element.40.sent), channel_id=1, source_target_pairs={{0,5},{1,2},{3,6},{2,1},{5,0},{4,7},{6,3},{7,4},{8,13},{9,10},{11,... | collective-permute-start | bytes 172040 | tf_op jit(solution)/shard_map/ppermute | solution.py:257
  9.1 1.6 %collective-permute-start.1 = (bf16[64,256]{1,0:T(8,128)(2,1)S(1)}, bf16[64,256]{1,0:T(8,128)(2,1)S(1)}, u32[]{:S(2)}, u32[]{:S(2)}) collective-permute-start(bf16[64,256]{1,0:T(8,128)(2,1)S(1)} %pad_maximum_fusion.2), channel_id=1, source_target_pairs={{0,8},{1,17},{8,0},{9,25},{16,24},{17,1},{24,16},{25,9},{2,10},{3,... | collective-permute-start | bytes 98312 | tf_op jit(solution)/shard_map/ppermute | solution.py:266
  10.7 0.9 %shard_map.123 = (f32[512,256]{1,0:T(8,128)S(1)}, f32[512,256]{1,0:T(8,128)S(1)}) custom-call(bf16[512,512]{1,0:T(8,128)(2,1)S(1)} %get-tuple-element.26.tgt_feats, bf16[512,256]{1,0:T(8,128)(2,1)S(1)} %get-tuple-element.27.w, f32[1,256]{1,0:T(1,128)S(1)} %get-tuple-element.28.bias, s32[1,4096]{1,0:T(1,128)S(1)} %get-tuple-element.29.e_tgt, ...), custom_call_target="tpu_custom_call" | custom-call | tf_op jit(solution)/shard_map/pallas_call | solution.py:240
  11.6 1.2 %shard_map.124 = (bf16[512,192]{1,0:T(8,128)(2,1)S(1)}, bf16[512,192]{1,0:T(8,128)(2,1)S(1)}, bf16[512,128]{1,0:T(8,128)(2,1)S(1)}, f32[512,256]{1,0:T(8,128)S(1)}) custom-call(f32[512,256]{1,0:T(8,128)S(1)} %get-tuple-element.31.acc, s32[1,4096]{1,0:T(1,128)S(1)} %get-tuple-element.29.e_tgt, s32[1,4096]{1,0:T(1,128)S(1)} %get-tuple-element.30.e_slot), custom_call_target="tpu_custom_call" | custom-call | tf_op jit(solution)/shard_map/pallas_call | solution.py:240
  12.8 0.0 collective-permute-done.3.got
  12.9 3.2 %collective-permute-start.4 = (bf16[112,256]{1,0:T(8,128)(2,1)S(1)}, bf16[112,256]{1,0:T(8,128)(2,1)S(1)}, u32[]{:S(2)}, u32[]{:S(2)}) collective-permute-start(bf16[112,256]{1,0:T(8,128)(2,1)S(1)} %get-tuple-element.43.sent), channel_id=1, source_target_pairs={{0,3},{1,4},{3,0},{2,7},{5,6},{4,1},{6,5},{7,2},{8,11},{9,12},{11,... | collective-permute-start | bytes 172040 | tf_op jit(solution)/shard_map/ppermute | solution.py:257
  16.1 0.0 collective-permute-done.1
  16.1 0.3 %shard_map.127 = (f32[512,256]{1,0:T(8,128)S(1)}, f32[16,256]{1,0:T(8,128)S(1)}) custom-call(bf16[512,192]{1,0:T(8,128)(2,1)S(1)} %get-tuple-element.32.hi, bf16[512,192]{1,0:T(8,128)(2,1)S(1)} %get-tuple-element.33.lo, f32[512,256]{1,0:T(8,128)S(1)} %get-tuple-element.34.own, f32[512,256]{1,0:T(8,128)S(1)} %get-tuple-element.35.scale, ...), custom_call_target="tpu_custom_call" | custom-call | tf_op jit(solution)/shard_map/pallas_call | solution.py:240
  16.4 1.5 %collective-permute-done.4.got = bf16[112,256]{1,0:T(8,128)(2,1)S(1)} collective-permute-done((bf16[112,256]{1,0:T(8,128)(2,1)S(1)}, bf16[112,256]{1,0:T(8,128)(2,1)S(1)}, u32[]{:S(2)}, u32[]{:S(2)}) %collective-permute-start.4) | collective-permute-done | bytes 57376 | tf_op jit(solution)/shard_map/ppermute | solution.py:257
  18.0 0.9 %shard_map.128 = (bf16[512,256]{1,0:T(8,128)(2,1)}, bf16[16,256]{1,0:T(8,128)(2,1)}) custom-call(f32[512,256]{1,0:T(8,128)S(1)} %get-tuple-element.45.mean, bf16[512,128]{1,0:T(8,128)(2,1)S(1)} %get-tuple-element.46.late, f32[512,256]{1,0:T(8,128)S(1)} %get-tuple-element.35.scale, bf16[112,256]{1,0:T(8,128)(2,1)S(1)} %collective-permute-done.4.got, ...), custom_call_target="tpu_custom_call" | custom-call | tf_op jit(solution)/shard_map/pallas_call | solution.py:240
  (7 shorter events, 0.1 us)
Async XLA Ops:
  2.4 6.0 %collective-permute-start = (bf16[64,256]{1,0:T(8,128)(2,1)S(1)}, bf16[64,256]{1,0:T(8,128)(2,1)S(1)}, u32[]{:S(2)}, u32[]{:S(2)}) collective-permute-start(bf16[64,256]{1,0:T(8,128)(2,1)S(1)} %pad_maximum_fusion.1), channel_id=1, source_target_pairs={{0,16},{1,9},{8,24},{9,1},{16,0},{17,25},{24,8},{25,17},{2,18},{3,... | collective-permute-start | bytes 98312 | tf_op jit(solution)/shard_map/ppermute | solution.py:266
  6.5 1.9 %collective-permute-start.2 = (bf16[160,256]{1,0:T(8,128)(2,1)S(1)}, bf16[160,256]{1,0:T(8,128)(2,1)S(1)}, u32[]{:S(2)}, u32[]{:S(2)}) collective-permute-start(bf16[160,256]{1,0:T(8,128)(2,1)S(1)} %get-tuple-element.37.sent), channel_id=1, source_target_pairs={{0,1},{1,0},{2,3},{3,2},{4,5},{5,4},{6,7},{7,6},{8,9},{9,8},{10,11... | collective-permute-start | bytes 245768 | tf_op jit(solution)/shard_map/ppermute | solution.py:323
  8.4 4.4 %collective-permute-start.3 = (bf16[112,256]{1,0:T(8,128)(2,1)S(1)}, bf16[112,256]{1,0:T(8,128)(2,1)S(1)}, u32[]{:S(2)}, u32[]{:S(2)}) collective-permute-start(bf16[112,256]{1,0:T(8,128)(2,1)S(1)} %get-tuple-element.40.sent), channel_id=1, source_target_pairs={{0,5},{1,2},{3,6},{2,1},{5,0},{4,7},{6,3},{7,4},{8,13},{9,10},{11,... | collective-permute-start | bytes 172040 | tf_op jit(solution)/shard_map/ppermute | solution.py:257
  9.1 6.9 %collective-permute-start.1 = (bf16[64,256]{1,0:T(8,128)(2,1)S(1)}, bf16[64,256]{1,0:T(8,128)(2,1)S(1)}, u32[]{:S(2)}, u32[]{:S(2)}) collective-permute-start(bf16[64,256]{1,0:T(8,128)(2,1)S(1)} %pad_maximum_fusion.2), channel_id=1, source_target_pairs={{0,8},{1,17},{8,0},{9,25},{16,24},{17,1},{24,16},{25,9},{2,10},{3,... | collective-permute-start | bytes 98312 | tf_op jit(solution)/shard_map/ppermute | solution.py:266
  12.9 5.1 %collective-permute-start.4 = (bf16[112,256]{1,0:T(8,128)(2,1)S(1)}, bf16[112,256]{1,0:T(8,128)(2,1)S(1)}, u32[]{:S(2)}, u32[]{:S(2)}) collective-permute-start(bf16[112,256]{1,0:T(8,128)(2,1)S(1)} %get-tuple-element.43.sent), channel_id=1, source_target_pairs={{0,3},{1,4},{3,0},{2,7},{5,6},{4,1},{6,5},{7,2},{8,11},{9,12},{11,... | collective-permute-start | bytes 172040 | tf_op jit(solution)/shard_map/ppermute | solution.py:257

commit v5 on v4

--- a/solution.py
+++ b/solution.py
@@ -20,13 +20,6 @@
     return bits
 
 
-def reverse_bits(value, bits):
-    out = value & 0
-    for i in range(bits):
-        out = out | (((value >> i) & 1) << (bits - 1 - i))
-    return out
-
-
 def one_hot(ids, rows):
     row = lax.broadcasted_iota(jnp.int32, (rows, ids.shape[1]), 0)
     return jnp.where(row == ids, 1.0, 0.0).astype(BF16)
@@ -57,9 +50,13 @@
     return out
 
 
-def places(n_hub):
-    z, h, c = lax.axis_index("blk"), lax.axis_index("hub"), lax.axis_index("rep")
-    return z, h, c, c ^ parity(h, bits_of(n_hub))
+def places():
+    return lax.axis_index("blk"), lax.axis_index("hub"), lax.axis_index("rep")
+
+
+def crossed(x, bits):
+    odd = parity(x, bits)
+    return jnp.where(x == 0, 0, 1 - odd) if isinstance(x, jax.Array) else int(x != 0) & (1 - odd)
 
 
 def project_kernel(
@@ -68,7 +65,7 @@
     src, w, send, hs, ht, lhs, sem,
 ):
     peers, n_hub, n_rep = sizes
-    z, h, c, side = places(n_hub)
+    z, h, c = places()
     copies = [
         pltpu.make_async_copy(a, b, sem.at[i])
         for i, (a, b) in enumerate(
@@ -90,16 +87,12 @@
     for copy in copies[:3]:
         copy.wait()
     for p in range(peers):
-        k = jnp.where((c & 1) == 1, p, reverse_bits(jnp.int32(p), bits_of(peers)))
-        row = send[0, pl.ds(k ^ z, 1), :]
+        row = send[0, pl.ds(p ^ z, 1), :]
         lhs[p * cap : (p + 1) * cap, :] = one_hot(row, sources).T
     target = ht[...]
     owner = target >> bits_of(per)
-    chip = owner >> 1
-    other = (owner & 1) ^ parity(chip, bits_of(n_hub))
-    x = chip ^ h
-    order = jnp.where(other == 1, reverse_bits(x, bits_of(n_hub)), x)
-    order = order | ((other ^ side) << bits_of(n_hub))
+    x = (owner >> 1) ^ h
+    order = x | (((owner & 1) ^ c ^ crossed(x, bits_of(n_hub))) << bits_of(n_hub))
     slot = (order << bits_of(per)) | (target & (per - 1))
     picks = one_hot(hs[...], sources)
     high, low = split_count(dot_nt(one_hot(slot, total), picks))
@@ -126,47 +119,36 @@
         copy.wait()
 
 
-def merge_kernel(got, sent, kept, cnt, *outs):
+def merge_kernel(got, sent, kept, cnt, mine, new_cnt, hubs, *messages):
     n = kept.shape[0]
+    per = mine.shape[0]
     sums = kept[...] + (got[:n].astype(F32) + got[n : 2 * n].astype(F32))
-    count_at = 2 * n
-    high = got[count_at : count_at + COUNT_ROWS].astype(F32)
+    mine[...] = sums[:per]
+    high = got[2 * n : 2 * n + COUNT_ROWS].astype(F32)
     counts = cnt[...] + (BASE * high[:8] + high[8:])
-    hubs_at = count_at + COUNT_ROWS
-    if len(outs) == 2:
-        keep, new_cnt = outs
-        keep[...] = sums
-        new_cnt[...] = counts
-        return
-    message, keep, new_cnt = outs
-    half = n // 2
-    keep[...] = sums[:half]
     new_cnt[...] = counts
-    high, low = split_sum(sums[half:])
-    message[:half, :] = high
-    message[half : 2 * half, :] = low
-    high, low = split_count(counts)
-    message[2 * half : 2 * half + COUNT_ROWS, :] = jnp.concatenate([high, low], axis=0)
-    rows = got.shape[0] - hubs_at
-    new_at = 2 * half + COUNT_ROWS
-    message[new_at : new_at + rows, :] = sent[hubs_at:, :]
-    message[new_at + rows :, :] = got[hubs_at:, :]
+    rows = jnp.concatenate([sent[2 * n + COUNT_ROWS :, :], got[2 * n + COUNT_ROWS :, :]], axis=0)
+    hubs[...] = rows
+    shared = jnp.concatenate([*split_count(counts), rows], axis=0)
+    for i, message in enumerate(messages):
+        high, low = split_sum(sums[(i + 1) * per : (i + 2) * per])
+        message[:per, :] = high
+        message[per : 2 * per, :] = low
+        message[2 * per :, :] = shared
 
 
 def edge_slots(sizes, cap, per, raw):
     peers, n_hub, _ = sizes
-    z, h, c, side = places(n_hub)
+    z, h, c = places()
     base = peers * cap
-    k = (raw >> bits_of(cap)) ^ z
-    k = jnp.where((c & 1) == 1, k, reverse_bits(k, bits_of(peers)))
-    low_slot = (k << bits_of(cap)) | (raw & (cap - 1))
+    low_slot = ((((raw >> bits_of(cap)) ^ z) << bits_of(cap)) | (raw & (cap - 1))) + (
+        (2 * n_hub) * per
+    )
     hub = raw - base
     owner = hub >> bits_of(per)
-    chip = owner >> 1
-    x = chip ^ h
-    x = jnp.where(side == 1, x, reverse_bits(x, bits_of(n_hub)))
-    q = (x << 1) | ((owner & 1) ^ parity(chip, bits_of(n_hub)) ^ side)
-    hub_slot = base + ((q << bits_of(per)) | (hub & (per - 1)))
+    x = (owner >> 1) ^ h
+    q = (x << 1) | ((owner & 1) ^ c ^ crossed(x, bits_of(n_hub)))
+    hub_slot = (q << bits_of(per)) | (hub & (per - 1))
     return jnp.where(raw < base, low_slot, hub_slot)
 
 
@@ -180,16 +162,11 @@
     return acc
 
 
-def own_kernel(sizes, cap, per, tgt_feats, w, bias, e_tgt, e_slot, own, acc):
+def count_kernel(sizes, cap, per, tgt_feats, w, bias, e_tgt, e_slot, own, hi, lo, late, scale):
     own[...] = dot_nn(tgt_feats[...], w[...]) + bias[...]
     slot = edge_slots(sizes, cap, per, e_slot[...])
-    acc[...] = edge_counts(*acc.shape, e_tgt[...], slot, 0, e_slot.shape[1] // 2)
-
-
-def count_kernel(sizes, cap, per, acc, e_tgt, e_slot, hi, lo, late, scale):
-    slot = edge_slots(sizes, cap, per, e_slot[...])
-    edges = e_slot.shape[1]
-    counts = acc[...] + edge_counts(*acc.shape, e_tgt[...], slot, edges // 2, edges)
+    slots = hi.shape[1] + late.shape[1] // 2
+    counts = edge_counts(own.shape[0], slots, e_tgt[...], slot, 0, e_slot.shape[1])
     early = hi.shape[1]
     high = jnp.floor(counts * (1.0 / BASE))
     low = counts - BASE * high
@@ -203,34 +180,41 @@
     scale[...] = jnp.broadcast_to(1.0 / degree, scale.shape)
 
 
-def blend_kernel(hi, lo, own, scale, rows, sent, hub, w, bias, mean, mine, table):
-    base = rows.shape[0]
-    table[:base, :] = rows[...]
-    table[base:, :] = sent[sent.shape[0] - (table.shape[0] - base) :, :]
+def blend_kernel(
+    sizes, hi, lo, own, scale, rows, hubs, kept, cnt, hub, w, bias, *rest
+):
+    _, n_hub, n_rep = sizes
+    _, h, c = places()
+    *gots, mean, hub_mean, table = rest
+    per = hub.shape[0]
+    pair = 2 * per
+    table[:pair, :] = hubs[...]
+    sums = kept[...]
+    counts = cnt[...]
+    for i, got in enumerate(gots):
+        table[(i + 1) * pair : (i + 2) * pair, :] = got[pair + COUNT_ROWS :, :]
+        sums = sums + (got[:per].astype(F32) + got[per:pair].astype(F32))
+        high = got[pair : pair + COUNT_ROWS].astype(F32)
+        counts = counts + (BASE * high[:8] + high[8:])
+    table[n_hub * pair :, :] = rows[...]
     values = table[...]
     neigh = BASE * dot_nn(hi[...], values) + dot_nn(lo[...], values)
     mean[...] = own[...] + neigh * scale[...]
-    mine[...] = dot_nn(hub[...], w[...]) + bias[...]
-
-
-def finish_kernel(sizes, mean, late, scale, got, kept, cnt, mine, out, hub_out):
-    _, n_hub, n_rep = sizes
-    _, h, c, _ = places(n_hub)
-    per = mine.shape[0]
-    hubs_at = 2 * per + COUNT_ROWS
-    rows = got[hubs_at:, :]
-    values = jnp.concatenate([rows, (BASE * rows.astype(F32)).astype(BF16)], axis=0)
-    neigh = dot_nn(late[...], values)
-    out[...] = jnp.maximum(mean[...] + neigh * scale[...], 0.0).astype(BF16)
-    sums = kept[...] + (got[:per].astype(F32) + got[per : 2 * per].astype(F32))
-    high = got[2 * per : 2 * per + COUNT_ROWS].astype(F32)
-    counts = cnt[...] + (BASE * high[:8] + high[8:])
     width = cnt.shape[1]
     row = lax.broadcasted_iota(jnp.int32, (per, width), 0)
     lane = lax.broadcasted_iota(jnp.int32, (per, width), 1)
     first = (h * n_rep + c) * per
     degree = jnp.sum(jnp.where(lane == row + first, counts[0:1, :], 0.0), axis=1, keepdims=True)
-    hub_out[...] = jnp.maximum(mine[...] + sums / jnp.maximum(degree, 1.0), 0.0).astype(BF16)
+    result = dot_nn(hub[...], w[...]) + sums / jnp.maximum(degree, 1.0) + bias[...]
+    hub_mean[...] = jnp.maximum(result, 0.0).astype(BF16)
+
+
+def finish_kernel(mean, late, scale, rows, hub_mean, out, hub_out):
+    values = rows[...]
+    values = jnp.concatenate([values, (BASE * values.astype(F32)).astype(BF16)], axis=0)
+    neigh = dot_nn(late[...], values)
+    out[...] = jnp.maximum(mean[...] + neigh * scale[...], 0.0).astype(BF16)
+    hub_out[...] = hub_mean[...]
 
 
 def call(kernel, out_shape, *args, mib=8, hbm=False, scratch=()):
@@ -247,23 +231,14 @@
     )(*args)
 
 
-def swap_hub(x, n_hub, step):
-    bits = bits_of(n_hub)
-    pairs = []
-    for h in range(n_hub):
-        for side in range(2):
-            to = h ^ (1 << (step if side == 1 else bits - 1 - step))
-            pairs.append((2 * h + (side ^ parity(h, bits)), 2 * to + (side ^ parity(to, bits))))
+def swap_hub(x, n_hub, bits):
+    flip = crossed(bits, bits_of(n_hub))
+    pairs = [(2 * h + c, 2 * (h ^ bits) + (c ^ flip)) for h in range(n_hub) for c in range(2)]
     return lax.ppermute(x, ("hub", "rep"), pairs)
 
 
 def swap_blk(x, peers, step):
-    pairs = []
-    for z in range(peers):
-        for c in range(2):
-            to = z ^ (1 << (step if c == 1 else bits_of(peers) - 1 - step))
-            pairs.append((2 * z + c, 2 * to + c))
-    return lax.ppermute(x, ("blk", "rep"), pairs)
+    return lax.ppermute(x, "blk", [(z, z ^ (1 << step)) for z in range(peers)])
 
 
 def on_device(
@@ -321,19 +296,18 @@
     )
 
     got = lax.ppermute(message, "rep", [(i, i ^ 1) for i in range(n_rep)])
-    for i in range(bits_of(n_hub)):
-        half = keep.shape[0] // 2
-        rows = got.shape[0] - 2 * keep.shape[0] - COUNT_ROWS
-        message, keep, cnt = call(
-            merge_kernel,
-            (
-                shape((2 * half + COUNT_ROWS + 2 * rows, width), BF16),
-                shape((half, width), F32),
-                shape((8, width), F32),
-            ),
-            got, message, keep, cnt,
-        )
-        got = swap_hub(message, n_hub, i)
+    wide = shape((4 * per + COUNT_ROWS, width), BF16)
+    keep, cnt, pair, *messages = call(
+        merge_kernel,
+        (
+            shape((per, width), F32),
+            shape((8, width), F32),
+            shape((2 * per, width), BF16),
+            *[wide] * (n_hub - 1),
+        ),
+        got, message, keep, cnt,
+    )
+    gots = [swap_hub(m, n_hub, i + 1) for i, m in enumerate(messages)]
 
     blocks = [outgoing[k * cap : (k + 1) * cap] for k in range(peers)]
     for i in range(bits_of(peers)):
@@ -342,33 +316,32 @@
         for j, k in enumerate(moved):
             blocks[k] = arrived[j * cap : (j + 1) * cap]
 
-    own, acc = call(
-        functools.partial(own_kernel, sizes, cap, per),
-        (shape((targets, width), F32), shape((targets, slots), F32)),
-        tgt, w_self, bias, e_tgt, e_slot, mib=24,
-    )
-    late_rows = group_hubs // 2
-    hi, lo, late, scale = call(
+    late_rows = peers * cap // 2
+    own, hi, lo, late, scale = call(
         functools.partial(count_kernel, sizes, cap, per),
         (
+            shape((targets, width), F32),
             shape((targets, slots - late_rows), BF16),
             shape((targets, slots - late_rows), BF16),
             shape((targets, 2 * late_rows), BF16),
             shape((targets, width), F32),
         ),
-        acc, e_tgt, e_slot, mib=24,
-    )
-    mean, mine = call(
-        blend_kernel,
-        (shape((targets, width), F32), shape((per, width), F32)),
-        hi, lo, own, scale, jnp.concatenate(blocks, axis=0), message, hubs, w_self, bias,
+        tgt, w_self, bias, e_tgt, e_slot,
+        mib=24,
+    )
+    mean, hub_mean = call(
+        functools.partial(blend_kernel, sizes),
+        (shape((targets, width), F32), shape((per, width), BF16)),
+        hi, lo, own, scale, jnp.concatenate(blocks[: peers // 2], axis=0), pair, keep, cnt,
+        hubs, w_self, bias, *gots,
         mib=24 if slots > 1024 else 8,
         scratch=[pltpu.VMEM((slots - late_rows, width), BF16)],
     )
     return call(
-        functools.partial(finish_kernel, sizes),
+        finish_kernel,
         (shape((targets, width), BF16), shape((per, width), BF16)),
-        mean, late, scale, got, keep, cnt, mine,
+        mean, late, scale, arrived, hub_mean,
+        mib=24 if slots > 1024 else 8,
     )
 
 

time: 19.2 us -> 19.3 us (level)
  waiting for transfers between devices: 3.44 us -> 4.33 us
  starting transfers between devices: 9.66 us -> 9.29 us
  Pallas kernels: 5.07 us -> 4.82 us
    ppermute x2 -> x3, waiting for transfers between devices: 1.54 us -> 4.32 us  [swap_hub(): return lax.ppermute(x, ('hub', 'rep'), pairs)]
    ppermute x2, waiting for transfers between devices: 1.89 us -> 0.01 us  [swap_blk(): return lax.ppermute(x, 'blk', [(z, z ^ 1 << step) for z in range(peers)])]
    ppermute x2 -> x3, starting transfers between devices: 3.95 us -> 3.08 us  [swap_hub(): return lax.ppermute(x, ('hub', 'rep'), pairs)]
    ppermute x2, starting transfers between devices: 5.71 us -> 6.21 us  [swap_blk(): return lax.ppermute(x, 'blk', [(z, z ^ 1 << step) for z in range(peers)])]
    pallas_call x7 -> x5, Pallas kernels: 5.07 us -> 4.82 us  [call(): pl.pallas_call(kernel, out_shape=out_shape, in_specs=[spec] * len(args),...]
  transfers between devices with their start and end apart: 5 -> 6, of which waited for: 2 -> 3; matrix products, arithmetic and copies ran while one was open for 0% -> 0% of each run, Pallas kernels for 13% -> 11%
where the time goes in v5:
time: 19.3 us; the launch traced here: 19.2 us
  starting transfers between devices  9.29 us (48%)
  Pallas kernels  4.82 us (25%)
  waiting for transfers between devices  4.33 us (22%)
  between operations  0.7 us (4%)
    ppermute x2, starting transfers between devices, swap_blk(): return lax.ppermute(x, 'blk', [(z, z ^ 1 << step) for z in range(peers)])  6.21 us
    pallas_call x5, Pallas kernels, call(): pl.pallas_call(kernel, out_shape=out_shape, in_specs=[spec] * len(args),...  4.82 us
    ppermute x3, waiting for transfers between devices, swap_hub(): return lax.ppermute(x, ('hub', 'rep'), pairs)  4.32 us
    ppermute x3, starting transfers between devices, swap_hub(): return lax.ppermute(x, ('hub', 'rep'), pairs)  3.08 us
  transfers between devices with their start and end apart: 6, of which 3 were waited for; matrix products, arithmetic and copies ran while one was open for 0% of the time, Pallas kernels for 11%

profile of v5, /device:TPU:0, one launch (start us, length us, event | category | flops | bytes accessed | tf_op | source)
XLA Modules:
  0.0 19.2 jit_solution(11094924816752041198)
XLA Ops:
  0.6 1.7 %shard_map.122 = (bf16[128,256]{1,0:T(8,128)(2,1)S(1)}, bf16[160,256]{1,0:T(8,128)(2,1)S(1)}, f32[64,256]{1,0:T(8,128)S(1)}, f32[8,256]{1,0:T(8,128)S(1)}, s32[1...) custom-call(bf16[256,512]{1,0:T(8,128)(2,1)} %src_h.1, ...), custom_call_target="tpu_custom_call" | custom-call | tf_op jit(solution)/shard_map/pallas_call | solution.py:224
  2.4 3.1 %collective-permute-start = (bf16[64,256]{1,0:T(8,128)(2,1)S(1)}, bf16[64,256]{1,0:T(8,128)(2,1)S(1)}, u32[]{:S(2)}, u32[]{:S(2)}) collective-permute-start(bf16[64,256]{1,0:T(8,128)(2,1)S(1)} %pad_maximum_fusion), channel_id=1, source_target_pairs={{0,8},{8,0},{16,24},{24,16},{1,9},{9,1},{17,25},{25,17},{2,10},{10... | collective-permute-start | bytes 98312 | tf_op jit(solution)/shard_map/ppermute | solution.py:241
  5.5 0.0 collective-permute-start.1
  5.5 1.9 %shard_map.123 = (f32[512,256]{1,0:T(8,128)S(1)}, bf16[512,192]{1,0:T(8,128)(2,1)S(1)}, bf16[512,192]{1,0:T(8,128)(2,1)S(1)}, bf16[512,128]{1,0:T(8,128)(2,1)S(1)}, f32[512,256]{1,0:T(8,128)S(1)}) custom-call(bf16[512,512]{1,0:T(8,128)(2,1)S(1)} %get-tuple-element.25.tgt_feats, bf16[512,256]{1,0:T(8,128)(2,1)S(1)} %get-tuple-element.26.w, ...), custom_call_target="tpu_custom_call" | custom-call | tf_op jit(solution)/shard_map/pallas_call | solution.py:224
  7.4 0.0 collective-permute-done
  7.4 3.1 %collective-permute-start.5 = (bf16[64,256]{1,0:T(8,128)(2,1)S(1)}, bf16[64,256]{1,0:T(8,128)(2,1)S(1)}, u32[]{:S(2)}, u32[]{:S(2)}) collective-permute-start(bf16[64,256]{1,0:T(8,128)(2,1)S(1)} %pad_maximum_fusion.2), channel_id=1, source_target_pairs={{0,16},{8,24},{16,0},{24,8},{1,17},{9,25},{17,1},{25,9},{2,18},{10... | collective-permute-start | bytes 98312 | tf_op jit(solution)/shard_map/ppermute | solution.py:241
  10.5 0.0 collective-permute-done.1.got
  10.5 1.6 %collective-permute-start.2 = (bf16[80,256]{1,0:T(8,128)(2,1)S(1)}, bf16[80,256]{1,0:T(8,128)(2,1)S(1)}, u32[]{:S(2)}, u32[]{:S(2)}) collective-permute-start(bf16[80,256]{1,0:T(8,128)(2,1)S(1)} %get-tuple-element.42), channel_id=1, source_target_pairs={{0,2},{1,3},{2,0},{3,1},{4,6},{5,7},{6,4},{7,5},{8,10},{9,11},{10,... | collective-permute-start | bytes 122888 | tf_op jit(solution)/shard_map/ppermute | solution.py:237
  12.1 1.5 %collective-permute-start.3 = (bf16[80,256]{1,0:T(8,128)(2,1)S(1)}, bf16[80,256]{1,0:T(8,128)(2,1)S(1)}, u32[]{:S(2)}, u32[]{:S(2)}) collective-permute-start(bf16[80,256]{1,0:T(8,128)(2,1)S(1)} %get-tuple-element.43), channel_id=1, source_target_pairs={{0,4},{1,5},{2,6},{3,7},{4,0},{5,1},{6,2},{7,3},{8,12},{9,13},{10,... | collective-permute-start | bytes 122888 | tf_op jit(solution)/shard_map/ppermute | solution.py:237
  13.6 0.0 collective-permute-start.4
  13.6 1.0 %collective-permute-done.2.rest_0_ = bf16[80,256]{1,0:T(8,128)(2,1)S(1)} collective-permute-done((bf16[80,256]{1,0:T(8,128)(2,1)S(1)}, bf16[80,256]{1,0:T(8,128)(2,1)S(1)}, u32[]{:S(2)}, u32[]{:S(2)}) %collective-permute-start.2) | collective-permute-done | bytes 40992 | tf_op jit(solution)/shard_map/ppermute | solution.py:237
  14.6 1.5 %collective-permute-done.3.rest_1_ = bf16[80,256]{1,0:T(8,128)(2,1)S(1)} collective-permute-done((bf16[80,256]{1,0:T(8,128)(2,1)S(1)}, bf16[80,256]{1,0:T(8,128)(2,1)S(1)}, u32[]{:S(2)}, u32[]{:S(2)}) %collective-permute-start.3) | collective-permute-done | bytes 40992 | tf_op jit(solution)/shard_map/ppermute | solution.py:237
  16.1 1.8 %collective-permute-done.4.rest_2_ = bf16[80,256]{1,0:T(8,128)(2,1)S(1)} collective-permute-done((bf16[80,256]{1,0:T(8,128)(2,1)S(1)}, bf16[80,256]{1,0:T(8,128)(2,1)S(1)}, u32[]{:S(2)}, u32[]{:S(2)}) %collective-permute-start.4) | collective-permute-done | bytes 40992 | tf_op jit(solution)/shard_map/ppermute | solution.py:237
  17.9 0.3 %shard_map.125 = (f32[512,256]{1,0:T(8,128)S(1)}, bf16[16,256]{1,0:T(8,128)(2,1)S(1)}) custom-call(bf16[512,192]{1,0:T(8,128)(2,1)S(1)} %get-tuple-element.30.hi, bf16[512,192]{1,0:T(8,128)(2,1)S(1)} %get-tuple-element.31.lo, f32[512,256]{1,0:T(8,128)S(1)} %get-tuple-element.32.own, f32[512,256]{1,0:T(8,128)S(1)} %get-tuple-element.33.scale, ...), custom_call_target="tpu_custom_call" | custom-call | tf_op jit(solution)/shard_map/pallas_call | solution.py:224
  18.2 0.0 collective-permute-done.5.rows
  18.2 0.9 %shard_map.126 = (bf16[512,256]{1,0:T(8,128)(2,1)}, bf16[16,256]{1,0:T(8,128)(2,1)}) custom-call(f32[512,256]{1,0:T(8,128)S(1)} %get-tuple-element.45.mean, bf16[512,128]{1,0:T(8,128)(2,1)S(1)} %get-tuple-element.46.late, f32[512,256]{1,0:T(8,128)S(1)} %get-tuple-element.33.scale, bf16[64,256]{1,0:T(8,128)(2,1)S(1)} %collective-permute-done.5.rows, ...), custom_call_target="tpu_custom_call" | custom-call | tf_op jit(solution)/shard_map/pallas_call | solution.py:224
  (6 shorter events, 0.1 us)
Async XLA Ops:
  2.4 5.0 %collective-permute-start = (bf16[64,256]{1,0:T(8,128)(2,1)S(1)}, bf16[64,256]{1,0:T(8,128)(2,1)S(1)}, u32[]{:S(2)}, u32[]{:S(2)}) collective-permute-start(bf16[64,256]{1,0:T(8,128)(2,1)S(1)} %pad_maximum_fusion), channel_id=1, source_target_pairs={{0,8},{8,0},{16,24},{24,16},{1,9},{9,1},{17,25},{25,17},{2,10},{10... | collective-permute-start | bytes 98312 | tf_op jit(solution)/shard_map/ppermute | solution.py:241
  5.5 5.0 %collective-permute-start.1 = (bf16[160,256]{1,0:T(8,128)(2,1)S(1)}, bf16[160,256]{1,0:T(8,128)(2,1)S(1)}, u32[]{:S(2)}, u32[]{:S(2)}) collective-permute-start(bf16[160,256]{1,0:T(8,128)(2,1)S(1)} %get-tuple-element.35.sent), channel_id=1, source_target_pairs={{0,1},{1,0},{2,3},{3,2},{4,5},{5,4},{6,7},{7,6},{8,9},{9,8},{10,11... | collective-permute-start | bytes 245768 | tf_op jit(solution)/shard_map/ppermute | solution.py:298
  7.4 10.8 %collective-permute-start.5 = (bf16[64,256]{1,0:T(8,128)(2,1)S(1)}, bf16[64,256]{1,0:T(8,128)(2,1)S(1)}, u32[]{:S(2)}, u32[]{:S(2)}) collective-permute-start(bf16[64,256]{1,0:T(8,128)(2,1)S(1)} %pad_maximum_fusion.2), channel_id=1, source_target_pairs={{0,16},{8,24},{16,0},{24,8},{1,17},{9,25},{17,1},{25,9},{2,18},{10... | collective-permute-start | bytes 98312 | tf_op jit(solution)/shard_map/ppermute | solution.py:241
  10.5 4.1 %collective-permute-start.2 = (bf16[80,256]{1,0:T(8,128)(2,1)S(1)}, bf16[80,256]{1,0:T(8,128)(2,1)S(1)}, u32[]{:S(2)}, u32[]{:S(2)}) collective-permute-start(bf16[80,256]{1,0:T(8,128)(2,1)S(1)} %get-tuple-element.42), channel_id=1, source_target_pairs={{0,2},{1,3},{2,0},{3,1},{4,6},{5,7},{6,4},{7,5},{8,10},{9,11},{10,... | collective-permute-start | bytes 122888 | tf_op jit(solution)/shard_map/ppermute | solution.py:237
  12.1 4.0 %collective-permute-start.3 = (bf16[80,256]{1,0:T(8,128)(2,1)S(1)}, bf16[80,256]{1,0:T(8,128)(2,1)S(1)}, u32[]{:S(2)}, u32[]{:S(2)}) collective-permute-start(bf16[80,256]{1,0:T(8,128)(2,1)S(1)} %get-tuple-element.43), channel_id=1, source_target_pairs={{0,4},{1,5},{2,6},{3,7},{4,0},{5,1},{6,2},{7,3},{8,12},{9,13},{10,... | collective-permute-start | bytes 122888 | tf_op jit(solution)/shard_map/ppermute | solution.py:237
  13.6 4.3 %collective-permute-start.4 = (bf16[80,256]{1,0:T(8,128)(2,1)S(1)}, bf16[80,256]{1,0:T(8,128)(2,1)S(1)}, u32[]{:S(2)}, u32[]{:S(2)}) collective-permute-start(bf16[80,256]{1,0:T(8,128)(2,1)S(1)} %get-tuple-element.44), channel_id=1, source_target_pairs={{0,7},{1,6},{2,5},{3,4},{4,3},{5,2},{6,1},{7,0},{8,15},{9,14},{10,... | collective-permute-start | bytes 122888 | tf_op jit(solution)/shard_map/ppermute | solution.py:237
